TPU v7x, 32 devices: a whole 2x2x4 slice. The times are simulated.
32 devices in a mesh: groups: 2 (over y), tm: 4 (over z), rows: 4 (over x, core).
Axes of the slice: x: 2, y: 2, z: 4, core: 2. Of those that a mesh axis runs over, the one named last changes fastest.
Arguments:
- inputs: bfloat16 [8, 16, 4, 19968], P('groups', 'tm', 'rows'), parts along dimension 0, may hold values from -6 to 6
- cotangent: bfloat16 [8, 16, 4, 19968], P('groups', 'tm', 'rows'), parts along dimension 0, may hold values from -6 to 6
- kernel: bfloat16 [27, 192, 192], replicated, may hold values from -0.078125 to 0.078125
- span_frames: int32 [8], P('groups'), parts along dimension 0, may hold values from 1 to 4, as said below
Outputs:
- grad_inputs: bfloat16 [8, 16, 4, 19968], P('groups', 'tm', 'rows'), parts along dimension 0
- weight_grad: float32 [54, 192, 192], P('groups', 'tm', 'rows'), parts along dimension 0
There are 2 independent parts, one for each index of `groups`. A program takes and returns all parts, laid end to end along the dimension named above; an argument that names none is the same for every part. Nothing has to cross between parts.
Inputs may be any that keep to these rules, and one draw needn't show every extreme that they name: Entry 0 is 1. Time span c holds span_frames[c] consecutive frames of every video in its first slots, the frames following those of span c - 1; its other slots hold no frame, and inputs and cotangent there are not read.
All inputs are finite; a program needn't handle non-finite values.
Results may differ from a plain program's by a relative error of at most 0.0031.
Values may be sent and summed in bfloat16 or wider, within the bound.
A program may use at most 192 MiB of HBM per device.

v0:
```python
import jax
import jax.numpy as jnp
from jax import lax
from jax.sharding import PartitionSpec as P

CH = 192
GRID_W = 104


def carried_in(value, axis, join, neutral, backward):
    count, mine = (lax.axis_size(axis), lax.axis_index(axis))
    pieces = jax.tree.map(lambda part: lax.all_gather(part, axis), value)
    if backward:
        pieces = jax.tree.map(lambda part: part[::-1], pieces)
        mine = count - 1 - mine
    so_far = jax.tree.map(
        lambda part, zero: jnp.full_like(part, 0) + jnp.asarray(zero, part.dtype), value, neutral
    )

    def turn(position, so_far):
        longer = join(so_far, jax.tree.map(lambda part: part[position], pieces))
        return jax.tree.map(lambda new, old: jnp.where(position < mine, new, old), longer, so_far)

    return lax.fori_loop(0, count - 1, turn, so_far)


def padded(value, sides, width):
    for axis, dim in sides:
        count, length = (lax.axis_size(axis), value.shape[dim])
        up = [(i, (i + 1) % count) for i in range(count - 1)]
        down = [(j, i) for i, j in up]
        last = lax.slice_in_dim(value, length - width, length, axis=dim)
        leading = lax.slice_in_dim(value, 0, width, axis=dim)
        before = lax.ppermute(last, axis, up)
        after = lax.ppermute(leading, axis, down)
        value = jnp.concatenate([before, value, after], axis=dim)
    return value


def lookup(table, wanted):
    order = jnp.arange(table.shape[0], dtype=jnp.int32)
    return jnp.sum(jnp.where(order == wanted, table, 0))


def pick_slot(frames, wanted):
    limit = frames.shape[1] - 1
    return jnp.take(frames, jnp.clip(wanted, 0, limit), axis=1)


def join_past(earlier, later):
    early_frames, early_count = earlier
    late_frames, late_count = later
    newest = jnp.where(late_count == 0, early_frames[:, 1], late_frames[:, 1])
    oldest = jnp.where(
        late_count >= 2,
        late_frames[:, 0],
        jnp.where(late_count == 1, early_frames[:, 1], early_frames[:, 0]),
    )
    return (jnp.stack([oldest, newest], axis=1), jnp.minimum(early_count + late_count, 2))


def join_future(earlier, later):
    high_frames, high_count = earlier
    low_frames, low_count = later
    leading = jnp.where(low_count == 0, high_frames[:, 0], low_frames[:, 0])
    trailing = jnp.where(
        low_count >= 2,
        low_frames[:, 1],
        jnp.where(low_count == 1, high_frames[:, 0], high_frames[:, 1]),
    )
    return (jnp.stack([leading, trailing], axis=1), jnp.minimum(high_count + low_count, 2))


def body(inputs, cotangent, kernel, span_frames):
    batch, slots, strip, flat = inputs.shape
    position = lax.axis_index("tm")
    own_count = lookup(span_frames, position)
    values = inputs.astype(jnp.float32)
    sigma = jax.nn.sigmoid(values)
    silu_out = (values * sigma).astype(jnp.bfloat16)
    live = (jnp.arange(slots) < own_count)[None, :, None, None]
    grad_live = jnp.where(live, cotangent, jnp.zeros_like(cotangent))
    zero_frame = jnp.zeros_like(silu_out[:, 0])
    last_frame = pick_slot(silu_out, own_count - 1)
    second_last = jnp.where(own_count >= 2, pick_slot(silu_out, own_count - 2), zero_frame)
    mine_past = jnp.stack([second_last, last_frame], axis=1)
    short_count = jnp.minimum(own_count, 2)
    past_state = carried_in(
        (mine_past, short_count),
        "tm",
        join_past,
        (jnp.zeros_like(mine_past), jnp.zeros((), jnp.int32)),
        False,
    )
    before_two = past_state[0][:, 0]
    before_one = past_state[0][:, 1]
    mine_future = grad_live[:, :2]
    future_state = carried_in(
        (mine_future, short_count),
        "tm",
        join_future,
        (jnp.zeros_like(mine_future), jnp.zeros((), jnp.int32)),
        True,
    )
    after_one = future_state[0][:, 0]
    after_two = future_state[0][:, 1]
    extended_act = jnp.concatenate([before_two[:, None], before_one[:, None], silu_out], axis=1)
    base_grad = jnp.concatenate([grad_live, zero_frame[:, None], zero_frame[:, None]], axis=1)
    slot_order = jnp.arange(slots + 2, dtype=jnp.int32)[None, :, None, None]
    extended_grad = jnp.where(slot_order == own_count, after_one[:, None], base_grad)
    extended_grad = jnp.where(slot_order == own_count + 1, after_two[:, None], extended_grad)
    stacked = jnp.concatenate([extended_act, extended_grad], axis=1)
    rimmed = padded(stacked, (("rows", 2),), 1)
    rimmed = rimmed.reshape(batch, 2 * (slots + 2), strip + 2, GRID_W, CH)
    rimmed = jnp.pad(rimmed, ((0, 0), (0, 0), (0, 0), (1, 1), (0, 0)))
    act_pad = rimmed[:, : slots + 2]
    grad_pad = rimmed[:, slots + 2 :]
    grad_flat = grad_live.reshape(-1, CH)
    cell_count = grad_flat.shape[0]
    adjoint = jnp.zeros((cell_count, CH), jnp.float32)
    pieces = []
    for frame_off in range(3):
        for row_off in range(3):
            for col_off in range(3):
                tap_index = 9 * frame_off + 3 * row_off + col_off
                window = act_pad[
                    :,
                    frame_off : frame_off + slots,
                    row_off : row_off + strip,
                    col_off : col_off + GRID_W,
                ].reshape(cell_count, CH)
                pieces.append(
                    lax.dot_general(
                        window,
                        grad_flat,
                        (((0,), (0,)), ((), ())),
                        preferred_element_type=jnp.float32,
                    )
                )
                mirror = grad_pad[
                    :,
                    2 - frame_off : 2 - frame_off + slots,
                    2 - row_off : 2 - row_off + strip,
                    2 - col_off : 2 - col_off + GRID_W,
                ].reshape(cell_count, CH)
                adjoint = adjoint + lax.dot_general(
                    mirror,
                    kernel[tap_index],
                    (((1,), (1,)), ((), ())),
                    preferred_element_type=jnp.float32,
                )
    slope = sigma * (1.0 + values * (1.0 - sigma))
    product = adjoint.reshape(batch, slots, strip, flat) * slope
    grad_inputs = jnp.where(live, product, jnp.zeros_like(product)).astype(jnp.bfloat16)
    time_count = lax.axis_size("tm")
    strip_count = lax.axis_size("rows")
    total_cells = batch * slots * time_count * strip * strip_count * GRID_W
    factor = float(total_cells) ** (-0.5)
    partial_grad = jnp.stack(pieces) * factor
    spread = lax.psum_scatter(partial_grad, "tm", scatter_dimension=1, tiled=True)
    shares = lax.psum_scatter(spread, "rows", scatter_dimension=2, tiled=True)
    return (grad_inputs, shares)


def solution(mesh):
    return jax.shard_map(
        body,
        mesh=mesh,
        in_specs=(
            P("groups", "tm", "rows", None),
            P("groups", "tm", "rows", None),
            P(),
            P("groups"),
        ),
        out_specs=(P("groups", "tm", "rows", None), P("groups", "tm", "rows")),
        check_vma=False,
    )
```

profile of v0, /device:TPU:0, one launch (start us, length us, event | category | flops | bytes accessed | tf_op | source)
XLA Modules:
  0.0 574.6 jit_solution(11462911806862401477)
XLA Ops:
  18.7 10.4 %all-reduce.2 = s32[4]{0:T(128)S(1)} all-reduce(s32[4]{0:T(128)S(1)} %dynamic-update-slice.1), channel_id=1, replica_groups=mesh['groups'=2,'tm'=4,'rows'=4] {'tm'}, use_global_device_ids=true, to_apply=%add.2 | all-reduce | flops 4 | bytes 32
  29.2 17.8 %all-gather.7.cloned.1.call-done = bf16[16,2,1,19968]{3,1,2,0:T(2,128)(2,1)} async-done(((bf16[4,2,1,19968]{3,1,2,0:T(2,128)(2,1)}), bf16[16,2,1,19968]{3,1,2,0:T(2,128)(2,1)}) %all-gather.7.cloned.1.call-update) | async-done | bytes 1277968 | tf_op jit(solution)/shard_map/all_gather | solution.py:12
  47.0 3.2 rev.7
  50.2 18.3 %while.30 = (s32[]{:T(128)}, bf16[4,2,1,19968]{3,1,0,2:T(2,128)(2,1)S(1)}, s32[]{:T(128)}, s32[4]{0:T(128)S(1)}, bf16[4,4,2,1,19968]{4,2,1,3,0:T(2,128)(2,1)}, /...) while((s32[]{:T(128)}, bf16[4,2,1,19968]{3,1,0,2:T(2,128)(2,1)S(1)}, ...), condition=%wide.region_4.6_spmd.clone, body=%wide.region_3.5_spmd.clone.sunk | while | flops 1357831 | bytes 3195056 | solution.py:24
  69.0 11.2 %all-gather.5.cloned.1.call-done = bf16[16,2,1,19968]{3,1,2,0:T(2,128)(2,1)} async-done(((bf16[4,2,1,19968]{3,1,2,0:T(2,128)(2,1)}), bf16[16,2,1,19968]{3,1,2,0:T(2,128)(2,1)}) %all-gather.5.cloned.1.call-update) | async-done | bytes 1277968 | tf_op jit(solution)/shard_map/all_gather | solution.py:12
  80.2 18.3 %while.29 = (s32[]{:T(128)}, bf16[4,2,1,19968]{3,1,0,2:T(2,128)(2,1)S(1)}, s32[]{:T(128)}, s32[4]{0:T(128)S(1)}, bf16[4,4,2,1,19968]{4,2,1,3,0:T(2,128)(2,1)}, /...) while((s32[]{:T(128)}, bf16[4,2,1,19968]{3,1,0,2:T(2,128)(2,1)S(1)}, ...), condition=%wide.region_2.4_spmd.clone, body=%wide.region_1.3_spmd.clone.sunk | while | flops 1357831 | bytes 3195056 | solution.py:24
  103.1 4.6 collective-permute-start
  110.0 7.8 %pad_maximum_fusion = bf16[4,12,3,19968]{3,0,2,1:T(4,128)(2,1)} fusion(bf16[4,12,1,19968]{3,0,2,1:T(4,128)(2,1)} %collective-permute-done.1, bf16[4,6,1,19968]{3,0,2,1:T(4,128)(2,1)S(1)} %select_select_fusion, bf16[4,4,1,19968]{3,0,2,1:T(4,128)(2,1)S(1)} %fusion.3, bf16[4,2,1,19968]{3,0,2,1:T(4,128)(2,1)S(1)} %copy.88, ...), kind=kLoop, calls=%fused_computation.12 | loop fusion | flops 11501568 | bytes 11501568 | tf_op jit(solution)/shard_map/concatenate | solution.py:36
  117.8 12.6 %reshape.246 = bf16[4,12,3,104,192]{4,3,0,2,1:T(8,128)(2,1)} reshape(bf16[4,12,3,19968]{3,0,2,1:T(4,128)(2,1)} %pad_maximum_fusion) | data formatting | bytes 11501568 | tf_op jit(solution)/shard_map/reshape | solution.py:114
  130.4 8.0 %fusion.93 = (bf16[4,4,1,104,192]{4,3,0,2,1:T(8,128)(2,1)S(1)}, bf16[4,4,1,104,192]{4,3,0,2,1:T(8,128)(2,1)S(1)}, bf16[4,4,1,104,192]{4,3,0,2,1:T(8,128)(2,1)S(1...) fusion(bf16[4,12,3,104,192]{4,3,0,2,1:T(8,128)(2,1)} %reshape.246), kind=kLoop, calls=%fused_computation.211 | loop fusion | bytes 26198016 | tf_op jit(solution)/shard_map/slice | solution.py:126
  139.9 5.0 pad_slice_fusion
  144.9 4.5 pad_slice_fusion.1
  149.4 4.3 pad_slice_fusion.2
  153.7 4.1 pad_slice_fusion.3
  160.1 3.2 reshape.247
  165.6 3.2 reshape.248
  171.1 11.7 %reshape.249 = bf16[1664,192]{0,1:T(8,128)(2,1)} reshape(bf16[4,4,1,104,192]{3,1,0,4,2:T(4,128)(2,1)} %copy.91) | data formatting | bytes 1277952 | tf_op jit(solution)/shard_map/reshape | solution.py:145
  185.1 3.2 reshape.250
  190.6 3.2 reshape.251
  196.1 3.2 reshape.252
  201.5 3.2 reshape.253
  207.0 3.2 reshape.254
  212.5 3.2 reshape.255
  229.1 3.2 reshape.258
  234.7 3.2 reshape.259
  251.1 3.6 reshape.262
  257.0 3.2 reshape.263
  262.5 3.2 reshape.264
  268.0 3.2 reshape.265
  273.6 3.2 reshape.266
  279.1 3.2 reshape.267
  284.6 3.2 reshape.268
  295.7 3.2 reshape.270
  301.2 3.2 reshape.271
  306.7 3.2 reshape.272
  312.2 3.2 reshape.273
  317.7 3.2 reshape.275
  322.2 3.5 reshape.277
  327.9 3.2 reshape.278
  332.5 3.3 reshape.279
  337.1 3.3 reshape.280
  341.7 3.2 reshape.281
  377.2 3.3 reshape.294
  381.9 3.3 reshape.295
  386.5 3.3 reshape.296
  439.9 92.6 %reduce-scatter.5.cloned.1.call-done = f32[27,48,192]{2,1,0:T(8,128)} async-done(((f32[27,192,192]{2,1,0:T(8,128)}), f32[27,48,192]{2,1,0:T(8,128)}) %reduce-scatter.5.cloned.1.call-update) | async-done | bytes 995344 | tf_op jit(solution)/shard_map/reduce_scatter | solution.py:160
  532.5 4.6 copy.147
  542.9 22.1 %reduce-scatter.7.cloned.1.call-done = f32[48,1296]{1,0:T(8,128)} async-done(((f32[192,1296]{1,0:T(8,128)}), f32[48,1296]{1,0:T(8,128)}) %reduce-scatter.7.cloned.1.call-update) | async-done | bytes 248848
  (363 shorter events, 222.4 us)
Async XLA Ops:
  7.2 4.6 copy-start.24
  7.2 39.8 %all-gather.7.cloned.1.call-start = ((), (), s32[]{:S(2)}) async-start(), calls=%async_computation.4 | async-start | bytes 1597440 | tf_op jit(solution)/shard_map/all_gather | solution.py:12
  10.6 6.8 %copy-start.78 = (u32[32]{0:T(128)S(1)}, u32[32]{0:T(128)}, u32[]{:S(2)}) copy-start(u32[32]{0:T(128)} %constant.136) | copy-start | bytes 388
  11.7 68.4 %all-gather.5.cloned.1.call-start = ((), (), s32[]{:S(2)}) async-start(), calls=%async_computation.3 | async-start | bytes 1597440 | tf_op jit(solution)/shard_map/all_gather | solution.py:12
  15.6 516.9 %reduce-scatter.5.cloned.1.call-start = ((), (), s32[]{:S(2)}) async-start(), calls=%async_computation.2 | async-start | bytes 6635520 | tf_op jit(solution)/shard_map/reduce_scatter | solution.py:160
  101.8 6.9 %collective-permute-start.1 = (bf16[4,12,1,19968]{3,0,2,1:T(4,128)(2,1)}, bf16[4,12,1,19968]{3,0,2,1:T(4,128)(2,1)}, u32[]{:S(2)}, u32[]{:S(2)}) collective-permute-start(bf16[4,12,1,19968]{3,0,2,1:T(4,128)(2,1)} %pad_maximum_fusion.1), channel_id=1, source_target_pairs={{1,0},{2,1},{3,2},{5,4},{6,5},{7,6},{9,8},{10,9},{11,10},{13,12},{... | collective-permute-start | bytes 5750792 | tf_op jit(solution)/shard_map/ppermute | solution.py:35
  103.1 6.9 %collective-permute-start = (bf16[4,12,1,19968]{3,0,2,1:T(4,128)(2,1)}, bf16[4,12,1,19968]{3,0,2,1:T(4,128)(2,1)}, u32[]{:S(2)}, u32[]{:S(2)}) collective-permute-start(bf16[4,12,1,19968]{3,0,2,1:T(4,128)(2,1)} %pad_maximum_fusion.1), channel_id=1, source_target_pairs={{0,1},{1,2},{2,3},{4,5},{5,6},{6,7},{8,9},{9,10},{10,11},{12,13},{... | collective-permute-start | bytes 5750792 | tf_op jit(solution)/shard_map/ppermute | solution.py:34
  130.4 9.5 %copy-start = (bf16[4,12,3,104,192]{4,3,0,2,1:T(8,128)(2,1)S(1)}, bf16[4,12,3,104,192]{4,3,0,2,1:T(8,128)(2,1)}, u32[]{:S(2)}) copy-start(bf16[4,12,3,104,192]{4,3,0,2,1:T(8,128)(2,1)} %reshape.246) | copy-start | bytes 17252356
  322.2 8.9 %copy-start.22 = (bf16[4,4,1,104,192]{4,3,0,2,1:T(8,128)(2,1)S(1)}, bf16[4,4,1,104,192]{4,3,0,2,1:T(8,128)(2,1)}, u32[]{:S(2)}) copy-start(bf16[4,4,1,104,192]{4,3,0,2,1:T(8,128)(2,1)} %get-tuple-element.314) | copy-start | bytes 1916932
  332.5 7.9 %copy-start.21 = (bf16[4,4,1,104,192]{4,3,0,2,1:T(8,128)(2,1)S(1)}, bf16[4,4,1,104,192]{4,3,0,2,1:T(8,128)(2,1)}, u32[]{:S(2)}) copy-start(bf16[4,4,1,104,192]{4,3,0,2,1:T(8,128)(2,1)} %get-tuple-element.315) | copy-start | bytes 1916932
  337.1 7.8 %copy-start.20 = (bf16[4,4,1,104,192]{4,3,0,2,1:T(8,128)(2,1)S(1)}, bf16[4,4,1,104,192]{4,3,0,2,1:T(8,128)(2,1)}, u32[]{:S(2)}) copy-start(bf16[4,4,1,104,192]{4,3,0,2,1:T(8,128)(2,1)} %get-tuple-element.316) | copy-start | bytes 1916932
  345.6 4.3 copy-start.19
  348.1 4.8 copy-start.17
  351.1 4.4 copy-start.18
  353.6 4.4 copy-start.16
  356.1 4.4 copy-start.15
  358.7 4.4 copy-start.14
  361.2 4.4 copy-start.13
  363.7 4.4 copy-start.12
  366.3 4.4 copy-start.11
  368.8 4.4 copy-start.10
  371.4 4.5 copy-start.9
  374.0 6.5 %copy-start.6 = (bf16[4,4,1,104,192]{4,3,0,2,1:T(8,128)(2,1)S(1)}, bf16[4,4,1,104,192]{4,3,0,2,1:T(8,128)(2,1)}, u32[]{:S(2)}) copy-start(bf16[4,4,1,104,192]{4,3,0,2,1:T(8,128)(2,1)} %get-tuple-element.319) | copy-start | bytes 1916932
  377.2 7.9 %copy-start.8 = (bf16[4,4,1,104,192]{4,3,0,2,1:T(8,128)(2,1)S(1)}, bf16[4,4,1,104,192]{4,3,0,2,1:T(8,128)(2,1)}, u32[]{:S(2)}) copy-start(bf16[4,4,1,104,192]{4,3,0,2,1:T(8,128)(2,1)} %get-tuple-element.327) | copy-start | bytes 1916932
  381.9 7.9 %copy-start.7 = (bf16[4,4,1,104,192]{4,3,0,2,1:T(8,128)(2,1)S(1)}, bf16[4,4,1,104,192]{4,3,0,2,1:T(8,128)(2,1)}, u32[]{:S(2)}) copy-start(bf16[4,4,1,104,192]{4,3,0,2,1:T(8,128)(2,1)} %get-tuple-element.320) | copy-start | bytes 1916932
  386.5 5.8 %copy-start.4 = (bf16[4,4,1,104,192]{4,3,0,2,1:T(8,128)(2,1)S(1)}, bf16[4,4,1,104,192]{4,3,0,2,1:T(8,128)(2,1)}, u32[]{:S(2)}) copy-start(bf16[4,4,1,104,192]{4,3,0,2,1:T(8,128)(2,1)} %get-tuple-element.309) | copy-start | bytes 1916932
  390.5 4.4 copy-start.5
  393.0 4.4 copy-start.3
  395.6 4.4 copy-start.2
  398.1 4.5 copy-start.1
  402.7 2.5 copy-start.51
  403.4 2.2 copy-start.52
  405.2 1.4 copy-start.54
  405.6 1.5 copy-start.55
  407.0 1.2 copy-start.58
  407.8 1.2 copy-start.60
  408.2 1.2 copy-start.61
  408.6 1.2 copy-start.62
  409.4 1.2 copy-start.64
  409.8 1.2 copy-start.65
  411.4 1.2 copy-start.69
  412.5 1.2 copy-start.72
  412.9 1.2 copy-start.73
  413.3 1.2 copy-start.74
  418.8 1.7 copy-start.23
  418.8 3.2 copy-start.25
  418.9 146.1 %reduce-scatter.7.cloned.1.call-start = ((), (), s32[]{:S(2)}) async-start(), calls=%async_computation.5 | async-start | bytes 1351680
  420.6 1.8 copy-start.26
  (37 other events, 42.3 us)
Sparse Core Ops, SparseCore 0:
  11.9 35.0 all-gather.6
  49.1 31.0 all-gather.4
  419.0 113.4 reduce-scatter.4
  539.3 25.6 reduce-scatter.6
where the time goes:
time: 586 us; the launch traced here: 575 us
  local copies, waits for them, and re-layouts  327 us (56%)
  waiting for transfers between devices  145 us (25%)
  other arithmetic  35.3 us (6%)
  matrix products  20.5 us (3%)
  between operations  18.3 us (3%)
  loops' own time  11.9 us (2%)
  blocking collectives  10.4 us (2%)
  starting transfers between devices  6.25 us (1%)
    reshape x27, local copies, waits for them, and re-layouts, body(): mirror = grad_pad[:, 2 - frame_off:2 - frame_off + slots, 2 - row_off:2 -...  95.7 us
    reduce_scatter x1, waiting for transfers between devices, body(): lax.psum_scatter(partial_grad, 'tm', scatter_dimension=1, tiled=True)  92.6 us
    reshape x27, local copies, waits for them, and re-layouts, body(): window = act_pad[:, frame_off:frame_off + slots, row_off:row_off + strip,...  62.2 us
    slice x27, local copies, waits for them, and re-layouts, body(): grad_pad[:, 2 - frame_off:2 - frame_off + slots, 2 - row_off:2 - row_off...  61.9 us
    slice x32, local copies, waits for them, and re-layouts, body(): act_pad[:, frame_off:frame_off + slots, row_off:row_off + strip, col_off:...  53.1 us
    all_gather x2, waiting for transfers between devices, carried_in(): pieces = jax.tree.map(lambda part: lax.all_gather(part, axis), value)  29 us
    unnamed x5, waiting for transfers between devices  22.1 us
    unnamed x166, local copies, waits for them, and re-layouts  21.3 us
  transfers between devices with their start and end apart: 6, of which 5 were waited for; matrix products, arithmetic and copies ran while one was open for 7% of the time, Pallas kernels for 0%

commit v1 on v0

v1 whole, which is shorter than its diff:
```python
import functools

import jax
import jax.numpy as jnp
from jax import lax
from jax.experimental import pallas as pl
from jax.experimental.pallas import tpu as pltpu
from jax.sharding import PartitionSpec as P

CH = 192
PAIR = 2 * CH
MESH = pl.DeviceIdType.MESH


def local_kernel(cells, strips, x_ref, mask_ref, grad_ref, kern_ref, out_ref, wg_ref, xc, act, act3, gc):
    frames = x_ref.shape[0]
    pairs = cells // 2
    wide = CH // strips
    live = mask_ref[...] > 0.5

    def split(p, carry):
        at = pl.multiple_of(p * PAIR, 128)
        v = x_ref[:, pl.ds(at, PAIR)]
        for q in range(2):
            cell = v[:, q * CH:(q + 1) * CH]
            xc[2 * p + q] = cell
            xf = cell.astype(jnp.float32)
            s = 1.0 / (1.0 + jnp.exp(-xf))
            act[2 * p + q + 1] = jnp.where(live, xf * s, 0.0).astype(jnp.bfloat16)
        for k in range(9):
            g = grad_ref[k, :, pl.ds(at, PAIR)]
            gc[k, 2 * p + 1] = g[:, :CH]
            gc[k, 2 * p + 2] = g[:, CH:]
        return carry

    zero = jnp.zeros((frames, CH), jnp.bfloat16)
    for end in (0, cells + 1):
        act[end] = zero
        for k in range(9):
            gc[k, end] = zero
    lax.fori_loop(0, pairs, split, 0)

    def widen(w, carry):
        act3[w] = jnp.concatenate([act[w], act[w + 1], act[w + 2]], axis=1)
        return carry

    lax.fori_loop(0, cells, widen, 0)
    a3 = act3[...].reshape(cells * frames, 3 * CH)

    def weight(k, carry):
        g = gc[k, pl.ds(1, cells)].reshape(cells * frames, CH)
        res = lax.dot_general(g, a3, (((0,), (0,)), ((), ())), preferred_element_type=jnp.float32)
        for r in range(strips):
            wg_ref[r, k] = res[r * wide:(r + 1) * wide]
        return carry

    lax.fori_loop(0, 9, weight, 0)

    step = 26 if cells % 26 == 0 else 2

    def adjoint(j, carry):
        w0 = j * step
        acc = jnp.zeros((step * frames, CH), jnp.float32)
        for k in range(9):
            for c in range(3):
                g = gc[k, pl.ds(w0 + 2 - c, step)].reshape(step * frames, CH)
                acc = acc + lax.dot_general(
                    g, kern_ref[3 * k + c], (((1,), (1,)), ((), ())), preferred_element_type=jnp.float32
                )
        acc = acc.reshape(step, frames, CH)
        xf = xc[pl.ds(w0, step)].astype(jnp.float32)
        s = 1.0 / (1.0 + jnp.exp(-xf))
        res = jnp.where(live[None], acc * (s * (1.0 + xf * (1.0 - s))), 0.0).astype(jnp.bfloat16)
        for p in range(step // 2):
            at = pl.multiple_of((w0 + 2 * p) * CH, 128)
            out_ref[:, pl.ds(at, PAIR)] = jnp.concatenate([res[2 * p], res[2 * p + 1]], axis=1)
        return carry

    lax.fori_loop(0, cells // step, adjoint, 0)


def reduce_kernel(strips, spans, factor, wg_ref, out_ref, got1, send2, got2, zfull, zsend, got3, s1, r1, s2, r2, s3, r3):
    row = lax.axis_index("rows")
    span = lax.axis_index("tm")
    half = strips // 2
    place = row // 2
    parity = row - 2 * place
    other = 1 - parity
    partner = 2 * place + other
    part = CH // spans
    taps, wide = wg_ref.shape[1], wg_ref.shape[2]

    def strip_at(d):
        return lax.rem(place + d, half)

    barrier = pltpu.get_barrier_semaphore()
    pl.semaphore_signal(barrier, inc=1, device_id={"rows": partner}, device_id_type=MESH)
    for d in range(1, half):
        pl.semaphore_signal(barrier, inc=1, device_id={"rows": 2 * strip_at(d) + parity}, device_id_type=MESH)
    for d in range(1, spans):
        pl.semaphore_signal(barrier, inc=1, device_id={"tm": lax.rem(span + d, spans)}, device_id_type=MESH)
    pl.semaphore_wait(barrier, half + spans - 1)

    order = list(range(1, half)) + [0]
    first = []
    for d in order:
        k = strip_at(d)
        cp = pltpu.make_async_remote_copy(
            wg_ref.at[2 * k + other], got1.at[d], s1.at[d], r1.at[d],
            device_id={"rows": partner}, device_id_type=MESH,
        )
        cp.start()
        first.append(cp)
    second = []
    for d, cp in zip(order, first):
        cp.wait()
        if d:
            k = strip_at(d)
            send2[d - 1] = (wg_ref[2 * k + parity] + got1[d]).astype(jnp.bfloat16)
            nxt = pltpu.make_async_remote_copy(
                send2.at[d - 1], got2.at[d - 1], s2.at[d - 1], r2.at[d - 1],
                device_id={"rows": 2 * k + parity}, device_id_type=MESH,
            )
            nxt.start()
            second.append(nxt)
    total = wg_ref[row] + got1[0]
    for d, cp in enumerate(second):
        cp.wait()
        total = total + got2[d].astype(jnp.float32)
    turned = total.reshape(taps * wide, 3 * CH).T
    for t in range(spans):
        for c in range(3):
            piece = turned[c * CH + t * part:c * CH + (t + 1) * part]
            zfull[t, c] = piece
            zsend[t, c] = piece.astype(jnp.bfloat16)
    third = []
    for d in range(1, spans):
        to = lax.rem(span + d, spans)
        cp = pltpu.make_async_remote_copy(
            zsend.at[to], got3.at[d - 1], s3.at[d - 1], r3.at[d - 1],
            device_id={"tm": to}, device_id_type=MESH,
        )
        cp.start()
        third.append(cp)
    final = zfull[span]
    for d, cp in enumerate(third):
        cp.wait()
        final = final + got3[d].astype(jnp.float32)
    out_ref[...] = final * factor


def body(inputs, cotangent, kernel, span_frames):
    batch, slots, strip, flat = inputs.shape
    cells = flat // CH
    frames = batch * slots
    assert strip == 1 and cells % 2 == 0 and frames % 16 == 0
    spans, strips = lax.axis_size("tm"), lax.axis_size("rows")
    assert strips % 2 == 0 and CH % spans == 0 and CH % strips == 0
    span = lax.axis_index("tm")
    count = jnp.sum(jnp.where(jnp.arange(span_frames.shape[0], dtype=jnp.int32) == span, span_frames, 0))
    x = inputs.reshape(batch, slots, flat)
    cot = cotangent.reshape(batch, slots, flat)

    back = [(i + 1, i) for i in range(spans - 1)]
    after_one = lax.ppermute(cot[:, 0], "tm", back)
    after_two = lax.ppermute(jnp.where(count >= 2, cot[:, 1], after_one), "tm", back)
    order = jnp.arange(slots + 2, dtype=jnp.int32)[None, :, None]
    ext = jnp.pad(cot, ((0, 0), (0, 2), (0, 0)))
    ext = jnp.where(order < count, ext, jnp.zeros_like(ext))
    ext = jnp.where(order == count, after_one[:, None], ext)
    ext = jnp.where(order == count + 1, after_two[:, None], ext)
    up = [(i, i + 1) for i in range(strips - 1)]
    down = [(i + 1, i) for i in range(strips - 1)]
    above = lax.ppermute(ext, "rows", up)
    below = lax.ppermute(ext, "rows", down)
    rows = (below, ext, above)
    grads = jnp.stack([
        rows[b][:, 2 - a:2 - a + slots].reshape(frames, flat) for a in range(3) for b in range(3)
    ])
    live = jnp.broadcast_to((jnp.arange(slots, dtype=jnp.int32) < count)[None, :, None], (batch, slots, CH))
    mask = live.astype(jnp.float32).reshape(frames, CH)

    vmem = pl.BlockSpec(memory_space=pltpu.VMEM)
    wide, part = CH // strips, CH // spans
    grad_in, wg = pl.pallas_call(
        functools.partial(local_kernel, cells, strips),
        out_shape=(
            jax.ShapeDtypeStruct((frames, flat), jnp.bfloat16),
            jax.ShapeDtypeStruct((strips, 9, wide, 3 * CH), jnp.float32),
        ),
        in_specs=[vmem] * 4,
        out_specs=(vmem, vmem),
        scratch_shapes=[
            pltpu.VMEM((cells, frames, CH), jnp.bfloat16),
            pltpu.VMEM((cells + 2, frames, CH), jnp.bfloat16),
            pltpu.VMEM((cells, frames, 3 * CH), jnp.bfloat16),
            pltpu.VMEM((9, cells + 2, frames, CH), jnp.bfloat16),
        ],
        compiler_params=pltpu.CompilerParams(vmem_limit_bytes=52 << 20),
        name="local",
    )(x.reshape(frames, flat), mask, grads, kernel)

    half = strips // 2
    total_cells = batch * slots * spans * strip * strips * cells
    block = (9, wide, 3 * CH)
    zblock = (3, part, 9 * wide)
    dma = pltpu.SemaphoreType.DMA
    few, some = max(half - 1, 1), max(spans - 1, 1)
    share = pl.pallas_call(
        functools.partial(reduce_kernel, strips, spans, float(total_cells) ** -0.5),
        out_shape=jax.ShapeDtypeStruct(zblock, jnp.float32),
        in_specs=[vmem],
        out_specs=vmem,
        scratch_shapes=[
            pltpu.VMEM((half,) + block, jnp.float32),
            pltpu.VMEM((few,) + block, jnp.bfloat16),
            pltpu.VMEM((few,) + block, jnp.bfloat16),
            pltpu.VMEM((spans,) + zblock, jnp.float32),
            pltpu.VMEM((spans,) + zblock, jnp.bfloat16),
            pltpu.VMEM((some,) + zblock, jnp.bfloat16),
            dma((half,)), dma((half,)), dma((few,)), dma((few,)), dma((some,)), dma((some,)),
        ],
        compiler_params=pltpu.CompilerParams(
            vmem_limit_bytes=52 << 20, collective_id=0, has_side_effects=True
        ),
        name="reduce",
    )(wg)
    share = share.reshape(3, part, 9, wide).transpose(2, 0, 1, 3).reshape(27, part, wide)
    return grad_in.reshape(batch, slots, strip, flat), share


def solution(mesh):
    return jax.shard_map(
        body,
        mesh=mesh,
        in_specs=(
            P("groups", "tm", "rows", None),
            P("groups", "tm", "rows", None),
            P(),
            P("groups"),
        ),
        out_specs=(P("groups", "tm", "rows", None), P("groups", "tm", "rows")),
        check_vma=False,
    )
```

time: 586 us -> 135 us (0.23); the launches traced: 575 us -> 134 us
  local copies, waits for them, and re-layouts: 327 us -> 46.6 us
  waiting for transfers between devices: 145 us -> 8.37 us
  Pallas kernels: 0 us -> 66.8 us
  other arithmetic: 35.3 us -> 3.49 us
  matrix products: 20.5 us -> 0 us
  between operations: 18.3 us -> 2.09 us
  loops' own time: 11.9 us -> 0 us
  blocking collectives: 10.4 us -> 0 us
    reshape x57 -> x1, local copies, waits for them, and re-layouts: 173 us -> 0.98 us  [body(): return (grad_in.reshape(batch, slots, strip, flat), share)]
    slice x62 -> x12, local copies, waits for them, and re-layouts: 116 us -> 16.6 us  [body(): rows[b][:, 2 - a:2 - a + slots].reshape(frames, flat)]
    reduce_scatter x1 -> x0, waiting for transfers between devices: 92.6 us -> none  [body(): lax.psum_scatter(partial_grad, 'tm', scatter_dimension=1, tiled=True)]
    pallas_call x0 -> x2, Pallas kernels: none -> 66.8 us  [the longest x1 34.3 us: body(): pl.pallas_call(functools.partial(reduce_kernel, strips, spans, float(tota...]
    all_gather x2 -> x0, waiting for transfers between devices: 29 us -> none  [carried_in(): pieces = jax.tree.map(lambda part: lax.all_gather(part, axis), value)]
    unnamed x5 -> x0, waiting for transfers between devices: 22.1 us -> none
    dot_general x54 -> x0, matrix products: 20.5 us -> none  [the longest x27 11 us: body(): lax.dot_general(mirror, kernel[tap_index], (((1,), (1,)), ((), ())), pref...]
    another operation x1 -> x11, local copies, waits for them, and re-layouts: 0.97 us -> 15.8 us  [the longest x10 14.5 us: body(): jnp.stack([rows[b][:, 2 - a:2 - a + slots].reshape(frames, flat) for a in...]
  transfers between devices with their start and end apart: 6 -> 4, of which waited for: 5 -> 2; matrix products, arithmetic and copies ran while one was open for 7% -> 16% of each run, Pallas kernels for 0% -> 0%
where the time goes in v1:
time: 135 us; the launch traced here: 134 us
  Pallas kernels  66.8 us (49%)
  local copies, waits for them, and re-layouts  46.6 us (35%)
  waiting for transfers between devices  8.37 us (6%)
  starting transfers between devices  6.96 us (5%)
  other arithmetic  3.49 us (3%)
  between operations  2.09 us (2%)
    pallas_call x1, Pallas kernels, body(): pl.pallas_call(functools.partial(reduce_kernel, strips, spans, float(tota...  34.3 us
    pallas_call x1, Pallas kernels, body(): pl.pallas_call(functools.partial(local_kernel, cells, strips), out_shape=...  32.4 us
    slice x12, local copies, waits for them, and re-layouts, body(): rows[b][:, 2 - a:2 - a + slots].reshape(frames, flat)  16.6 us
    another operation x10, local copies, waits for them, and re-layouts, body(): jnp.stack([rows[b][:, 2 - a:2 - a + slots].reshape(frames, flat) for a in...  14.5 us
    unnamed x21, local copies, waits for them, and re-layouts  11.7 us
    ppermute x1, waiting for transfers between devices, body(): after_one = lax.ppermute(cot[:, 0], 'tm', back)  4.48 us
    ppermute x1, waiting for transfers between devices, body(): lax.ppermute(jnp.where(count >= 2, cot[:, 1], after_one), 'tm', back)  3.88 us
    ppermute x1, starting transfers between devices, body(): above = lax.ppermute(ext, 'rows', up)  3.08 us
  transfers between devices with their start and end apart: 4, of which 2 were waited for; matrix products, arithmetic and copies ran while one was open for 16% of the time, Pallas kernels for 0%

profile of v1, /device:TPU:0, one launch (start us, length us, event | category | flops | bytes accessed | tf_op | source)
XLA Modules:
  0.0 134.2 jit_solution(4857280012775774221)
XLA Ops:
  0.6 1.3 copy.35
  2.0 1.3 collective-permute-start
  3.3 1.3 fusion.1
  5.9 0.6 compare_convert_fusion
  6.6 4.5 %collective-permute-done = bf16[4,19968]{1,0:T(4,128)(2,1)S(1)} collective-permute-done((bf16[4,19968]{1,0:T(4,128)(2,1)S(1)}, bf16[4,19968]{1,0:T(4,128)(2,1)S(1)}, u32[]{:S(2)}, u32[]{:S(2)}) %collective-permute-start) | collective-permute-done | bytes 159776 | tf_op jit(solution)/shard_map/ppermute | solution.py:165
  11.1 0.1 fusion
  11.2 1.3 collective-permute-start.1
  12.6 1.2 reshape_reshape.3.x_ref
  13.8 0.7 iota_compare_fusion
  14.5 3.9 %collective-permute-done.1 = bf16[4,19968]{1,0:T(4,128)(2,1)S(1)} collective-permute-done((bf16[4,19968]{1,0:T(4,128)(2,1)S(1)}, bf16[4,19968]{1,0:T(4,128)(2,1)S(1)}, u32[]{:S(2)}, u32[]{:S(2)}) %collective-permute-start.1) | collective-permute-done | bytes 159776 | tf_op jit(solution)/shard_map/ppermute | solution.py:166
  18.3 0.8 select_select_fusion
  19.2 1.3 collective-permute-start.2
  20.5 1.5 %fusion.3 = (bf16[4,4,19968]{2,0,1:T(4,128)(2,1)}, bf16[4,4,19968]{2,0,1:T(4,128)(2,1)}, bf16[4,4,19968]{2,0,1:T(4,128)(2,1)S(1)}) fusion(bf16[4,6,19968]{2,0,1:T(4,128)(2,1)S(1)} %select_select_fusion), kind=kLoop, calls=%fused_computation.21 | loop fusion | bytes 3833856 | tf_op jit(solution)/shard_map/slice | solution.py:178
  22.0 3.1 %collective-permute-start.3 = (bf16[4,6,19968]{2,0,1:T(4,128)(2,1)S(1)}, bf16[4,6,19968]{2,0,1:T(4,128)(2,1)S(1)}, u32[]{:S(2)}, u32[]{:S(2)}) collective-permute-start(bf16[4,6,19968]{2,0,1:T(4,128)(2,1)S(1)} %select_select_fusion), channel_id=1, source_target_pairs={{0,1},{1,2},{2,3},{4,5},{5,6},{6,7},{8,9},{9,10},{10,11},{12,13},{... | collective-permute-start | bytes 2875400 | tf_op jit(solution)/shard_map/ppermute | solution.py:174
  25.1 1.1 copy.23
  26.2 2.1 %stack_reshape.28 = bf16[1,16,19968]{2,1,0:T(8,128)(2,1)} reshape(bf16[4,4,19968]{2,1,0:T(4,128)(2,1)} %copy.23) | data formatting | bytes 1277952 | tf_op jit(solution)/shard_map/stack;reshape | solution.py:177
  28.3 2.2 %copy.26 = bf16[4,4,19968]{2,1,0:T(4,128)(2,1)} copy(bf16[4,4,19968]{2,0,1:T(4,128)(2,1)} %get-tuple-element.16) | data formatting | bytes 1277952 | tf_op jit(solution)/shard_map/slice | solution.py:178
  30.4 2.1 %stack_reshape.31 = bf16[1,16,19968]{2,1,0:T(8,128)(2,1)} reshape(bf16[4,4,19968]{2,1,0:T(4,128)(2,1)} %copy.26) | data formatting | bytes 1277952 | tf_op jit(solution)/shard_map/stack;reshape | solution.py:177
  32.5 2.2 %copy.29 = bf16[4,4,19968]{2,1,0:T(4,128)(2,1)} copy(bf16[4,4,19968]{2,0,1:T(4,128)(2,1)} %get-tuple-element.15) | data formatting | bytes 1277952 | tf_op jit(solution)/shard_map/slice | solution.py:178
  34.7 2.1 %stack_reshape.34 = bf16[1,16,19968]{2,1,0:T(8,128)(2,1)} reshape(bf16[4,4,19968]{2,1,0:T(4,128)(2,1)} %copy.29) | data formatting | bytes 1277952 | tf_op jit(solution)/shard_map/stack;reshape | solution.py:177
  36.8 1.5 %fusion.4 = (bf16[4,4,19968]{2,0,1:T(4,128)(2,1)}, bf16[4,4,19968]{2,0,1:T(4,128)(2,1)}, bf16[4,4,19968]{2,0,1:T(4,128)(2,1)S(1)}) fusion(bf16[4,6,19968]{2,0,1:T(4,128)(2,1)S(1)} %collective-permute-done.2), kind=kLoop, calls=%fused_computation.22 | loop fusion | bytes 3833856 | tf_op jit(solution)/shard_map/slice | solution.py:178
  38.3 0.2 copy.22
  38.6 1.0 stack_reshape.27
  39.5 2.0 %constant_dynamic-update-slice_fusion.8 = bf16[9,16,19968]{2,1,0:T(8,128)(2,1)} fusion(bf16[1,16,19968]{2,1,0:T(8,128)(2,1)} %stack_reshape.27), kind=kLoop, calls=%fused_computation.13 | loop fusion | bytes 1277952
  41.6 1.6 %fusion.2 = (bf16[4,4,19968]{2,0,1:T(4,128)(2,1)}, bf16[4,4,19968]{2,0,1:T(4,128)(2,1)}, bf16[4,4,19968]{2,0,1:T(4,128)(2,1)S(1)}) fusion(bf16[4,6,19968]{2,0,1:T(4,128)(2,1)S(1)} %collective-permute-done.3), kind=kLoop, calls=%fused_computation.20 | loop fusion | bytes 3833856 | tf_op jit(solution)/shard_map/slice | solution.py:178
  43.1 0.2 copy.24
  43.4 1.0 stack_reshape.29
  44.4 0.2 copy.25
  44.7 1.0 stack_reshape.30
  45.6 1.4 %copy.27 = bf16[4,4,19968]{2,1,0:T(4,128)(2,1)S(1)} copy(bf16[4,4,19968]{2,0,1:T(4,128)(2,1)} %get-tuple-element.13) | data formatting | bytes 1277952 | tf_op jit(solution)/shard_map/slice | solution.py:178
  47.0 0.2 stack_reshape.32
  47.2 2.2 %copy.28 = bf16[4,4,19968]{2,1,0:T(4,128)(2,1)} copy(bf16[4,4,19968]{2,0,1:T(4,128)(2,1)} %get-tuple-element.18) | data formatting | bytes 1277952 | tf_op jit(solution)/shard_map/slice | solution.py:178
  49.4 2.1 %stack_reshape.33 = bf16[1,16,19968]{2,1,0:T(8,128)(2,1)} reshape(bf16[4,4,19968]{2,1,0:T(4,128)(2,1)} %copy.28) | data formatting | bytes 1277952 | tf_op jit(solution)/shard_map/stack;reshape | solution.py:177
  51.5 2.2 %copy.30 = bf16[4,4,19968]{2,1,0:T(4,128)(2,1)} copy(bf16[4,4,19968]{2,0,1:T(4,128)(2,1)} %get-tuple-element.12) | data formatting | bytes 1277952 | tf_op jit(solution)/shard_map/slice | solution.py:178
  53.7 2.1 %stack_reshape.35 = bf16[1,16,19968]{2,1,0:T(8,128)(2,1)} reshape(bf16[4,4,19968]{2,1,0:T(4,128)(2,1)} %copy.30) | data formatting | bytes 1277952 | tf_op jit(solution)/shard_map/stack;reshape | solution.py:177
  55.8 0.9 constant_dynamic-update-slice_fusion.7
  56.7 2.0 %constant_dynamic-update-slice_fusion.6 = bf16[9,16,19968]{2,1,0:T(8,128)(2,1)} fusion(bf16[9,16,19968]{2,1,0:T(8,128)(2,1)} %constant_dynamic-update-slice_fusion.7, bf16[1,16,19968]{2,1,0:T(8,128)(2,1)} %stack_reshape.29), kind=kLoop, calls=%fused_computation.11 | loop fusion | bytes 1277952
  58.7 2.0 %constant_dynamic-update-slice_fusion.5 = bf16[9,16,19968]{2,1,0:T(8,128)(2,1)} fusion(bf16[9,16,19968]{2,1,0:T(8,128)(2,1)} %constant_dynamic-update-slice_fusion.6, bf16[1,16,19968]{2,1,0:T(8,128)(2,1)} %stack_reshape.30), kind=kLoop, calls=%fused_computation.10 | loop fusion | bytes 1277952
  60.6 0.9 constant_dynamic-update-slice_fusion.4
  61.5 0.9 constant_dynamic-update-slice_fusion.3
  62.4 0.9 constant_dynamic-update-slice_fusion.2
  63.3 0.9 constant_dynamic-update-slice_fusion.1
  64.2 0.9 constant_dynamic-update-slice_fusion.grad_ref
  65.1 32.4 %local.1 = (bf16[16,19968]{1,0:T(8,128)(2,1)S(1)}, f32[4,9,48,576]{3,2,1,0:T(8,128)}) custom-call(bf16[16,19968]{1,0:T(8,128)(2,1)S(1)} %reshape_reshape.3.x_ref, f32[16,192]{1,0:T(8,128)S(1)} %broadcast_in_dim.57.mask_ref, bf16[9,16,19968]{2,1,0:T(8,128)(2,1)} %constant_dynamic-update-slice_fusion.grad_ref, bf16[27,192,192]{2,1,0:T(8,128)(2,1)} %kern_ref.1), custom_call_target="tpu_custom_call" | custom-call | tf_op jit(solution)/shard_map/local/pallas_call | solution.py:185
  97.6 34.3 %reduce.1 = f32[3,48,432]{2,1,0:T(8,128)S(1)} custom-call(f32[4,9,48,576]{3,2,1,0:T(8,128)} %get-tuple-element.5.wg_ref), custom_call_target="tpu_custom_call" | custom-call | tf_op jit(solution)/shard_map/reduce/pallas_call | solution.py:209
  131.9 0.2 copy.31
  132.2 1.1 copy.32
  133.3 1.0 reshape.40
  (19 shorter events, 0.2 us)
Async XLA Ops:
  2.0 9.0 %collective-permute-start = (bf16[4,19968]{1,0:T(4,128)(2,1)S(1)}, bf16[4,19968]{1,0:T(4,128)(2,1)S(1)}, u32[]{:S(2)}, u32[]{:S(2)}) collective-permute-start(bf16[4,19968]{1,0:T(4,128)(2,1)S(1)} %slice_bitcast_fusion), channel_id=1, source_target_pairs={{4,0},{8,4},{12,8},{5,1},{9,5},{13,9},{6,2},{10,6},{14,10},{7,3},{... | collective-permute-start | bytes 479240 | tf_op jit(solution)/shard_map/ppermute | solution.py:165
  11.2 7.2 %collective-permute-start.1 = (bf16[4,19968]{1,0:T(4,128)(2,1)S(1)}, bf16[4,19968]{1,0:T(4,128)(2,1)S(1)}, u32[]{:S(2)}, u32[]{:S(2)}) collective-permute-start(bf16[4,19968]{1,0:T(4,128)(2,1)S(1)} %fusion), channel_id=1, source_target_pairs={{4,0},{8,4},{12,8},{5,1},{9,5},{13,9},{6,2},{10,6},{14,10},{7,3},{... | collective-permute-start | bytes 479240 | tf_op jit(solution)/shard_map/ppermute | solution.py:166
  19.2 17.6 %collective-permute-start.2 = (bf16[4,6,19968]{2,0,1:T(4,128)(2,1)S(1)}, bf16[4,6,19968]{2,0,1:T(4,128)(2,1)S(1)}, u32[]{:S(2)}, u32[]{:S(2)}) collective-permute-start(bf16[4,6,19968]{2,0,1:T(4,128)(2,1)S(1)} %select_select_fusion), channel_id=1, source_target_pairs={{1,0},{2,1},{3,2},{5,4},{6,5},{7,6},{9,8},{10,9},{11,10},{13,12},{... | collective-permute-start | bytes 2875400 | tf_op jit(solution)/shard_map/ppermute | solution.py:175
  22.0 19.6 %collective-permute-start.3 = (bf16[4,6,19968]{2,0,1:T(4,128)(2,1)S(1)}, bf16[4,6,19968]{2,0,1:T(4,128)(2,1)S(1)}, u32[]{:S(2)}, u32[]{:S(2)}) collective-permute-start(bf16[4,6,19968]{2,0,1:T(4,128)(2,1)S(1)} %select_select_fusion), channel_id=1, source_target_pairs={{0,1},{1,2},{2,3},{4,5},{5,6},{6,7},{8,9},{9,10},{10,11},{12,13},{... | collective-permute-start | bytes 2875400 | tf_op jit(solution)/shard_map/ppermute | solution.py:174
  39.5 4.9 %copy-start.5 = (bf16[4,4,19968]{2,0,1:T(4,128)(2,1)S(1)}, bf16[4,4,19968]{2,0,1:T(4,128)(2,1)}, u32[]{:S(2)}) copy-start(bf16[4,4,19968]{2,0,1:T(4,128)(2,1)} %get-tuple-element.19) | copy-start | bytes 1916932
  43.4 12.4 %copy-start.2 = (bf16[1,16,19968]{2,1,0:T(8,128)(2,1)S(1)}, bf16[1,16,19968]{2,1,0:T(8,128)(2,1)}, u32[]{:S(2)}) copy-start(bf16[1,16,19968]{2,1,0:T(8,128)(2,1)} %stack_reshape.28) | copy-start | bytes 1916932
  45.6 15.0 %copy-start.1 = (bf16[1,16,19968]{2,1,0:T(8,128)(2,1)S(1)}, bf16[1,16,19968]{2,1,0:T(8,128)(2,1)}, u32[]{:S(2)}) copy-start(bf16[1,16,19968]{2,1,0:T(8,128)(2,1)} %stack_reshape.31) | copy-start | bytes 1916932
  49.4 13.9 %copy-start = (bf16[1,16,19968]{2,1,0:T(8,128)(2,1)S(1)}, bf16[1,16,19968]{2,1,0:T(8,128)(2,1)}, u32[]{:S(2)}) copy-start(bf16[1,16,19968]{2,1,0:T(8,128)(2,1)} %stack_reshape.34) | copy-start | bytes 1916932
  55.8 6.6 %copy-start.4 = (bf16[1,16,19968]{2,1,0:T(8,128)(2,1)S(1)}, bf16[1,16,19968]{2,1,0:T(8,128)(2,1)}, u32[]{:S(2)}) copy-start(bf16[1,16,19968]{2,1,0:T(8,128)(2,1)} %stack_reshape.33) | copy-start | bytes 1916932
  55.8 8.4 %copy-start.3 = (bf16[1,16,19968]{2,1,0:T(8,128)(2,1)S(1)}, bf16[1,16,19968]{2,1,0:T(8,128)(2,1)}, u32[]{:S(2)}) copy-start(bf16[1,16,19968]{2,1,0:T(8,128)(2,1)} %stack_reshape.35) | copy-start | bytes 1916932

commit v2 on v1

v2 whole, which is shorter than its diff:
```python
import functools

import jax
import jax.numpy as jnp
from jax import lax
from jax.experimental import pallas as pl
from jax.experimental.pallas import tpu as pltpu
from jax.sharding import PartitionSpec as P

CH = 192
PAIR = 2 * CH
MESH = pl.DeviceIdType.MESH

CUTS = ((0, 5), (5, 9))


def kernel_body(cells, strips, spans, factor, x_ref, mask_ref, below_ref, own_ref, above_ref, kern_ref,
                out_ref, share0_ref, share1_ref, xc, act, act3, gc, wg, got1, send2, got2,
                zfull0, zfull1, zsend0, zsend1, got30, got31, s1, r1, s2, r2, s3, r3):
    frames = x_ref.shape[0]
    tail = own_ref.shape[0] - frames
    batch = tail // 2
    pairs = cells // 2
    wide, part, half = CH // strips, CH // spans, strips // 2
    share, zfull, zsend, got3 = (share0_ref, share1_ref), (zfull0, zfull1), (zsend0, zsend1), (got30, got31)
    row = lax.axis_index("rows")
    span = lax.axis_index("tm")
    place = row // 2
    parity = row - 2 * place
    other = 1 - parity
    partner = 2 * place + other

    def strip_at(d):
        return lax.rem(place + d, half)

    barrier = pltpu.get_barrier_semaphore()
    pl.semaphore_signal(barrier, inc=1, device_id={"rows": partner}, device_id_type=MESH)
    for d in range(1, half):
        pl.semaphore_signal(barrier, inc=1, device_id={"rows": 2 * strip_at(d) + parity}, device_id_type=MESH)
    for d in range(1, spans):
        pl.semaphore_signal(barrier, inc=1, device_id={"tm": lax.rem(span + d, spans)}, device_id_type=MESH)

    live = mask_ref[...] > 0.5
    grads = (below_ref, own_ref, above_ref)

    def split(p, carry):
        at = pl.multiple_of(p * PAIR, 128)
        v = x_ref[:, pl.ds(at, PAIR)]
        for q in range(2):
            cell = v[:, q * CH:(q + 1) * CH]
            xc[2 * p + q] = cell
            xf = cell.astype(jnp.float32)
            s = 1.0 / (1.0 + jnp.exp(-xf))
            act[2 * p + q + 1] = jnp.where(live, xf * s, 0.0).astype(jnp.bfloat16)
        for b in range(3):
            v = grads[b][:, pl.ds(at, PAIR)]
            for q in range(2):
                cell = v[:, q * CH:(q + 1) * CH]
                for a in range(3):
                    lo = (2 - a) * batch
                    gc[3 * a + b, 2 * p + q + 1] = cell[lo:lo + frames]
        return carry

    zero = jnp.zeros((frames, CH), jnp.bfloat16)
    for end in (0, cells + 1):
        act[end] = zero
        for k in range(9):
            gc[k, end] = zero
    lax.fori_loop(0, pairs, split, 0)

    def widen(w, carry):
        act3[w] = jnp.concatenate([act[w], act[w + 1], act[w + 2]], axis=1)
        return carry

    lax.fori_loop(0, cells, widen, 0)
    order = list(range(1, half)) + [0]
    copies1, copies2, copies3 = {}, {}, {}

    def weight(k, carry):
        g = gc[k, pl.ds(1, cells)].reshape(cells * frames, CH)
        a3 = act3[...].reshape(cells * frames, 3 * CH)
        res = lax.dot_general(g, a3, (((0,), (0,)), ((), ())), preferred_element_type=jnp.float32)
        for r in range(strips):
            wg[r, k] = res[r * wide:(r + 1) * wide]
        return carry

    def start_core(n):
        k0, k1 = CUTS[n]
        copies1[n] = []
        for d in order:
            cp = pltpu.make_async_remote_copy(
                wg.at[2 * strip_at(d) + other, pl.ds(k0, k1 - k0)], got1.at[d, pl.ds(k0, k1 - k0)],
                s1.at[n, d], r1.at[n, d], device_id={"rows": partner}, device_id_type=MESH,
            )
            cp.start()
            copies1[n].append(cp)

    def start_rows(n):
        k0, k1 = CUTS[n]
        copies2[n] = []
        for d, cp in zip(order, copies1[n]):
            cp.wait()
            if d:
                to = 2 * strip_at(d) + parity
                send2[d - 1, k0:k1] = (wg[to, k0:k1] + got1[d, k0:k1]).astype(jnp.bfloat16)
                nxt = pltpu.make_async_remote_copy(
                    send2.at[d - 1, pl.ds(k0, k1 - k0)], got2.at[d - 1, pl.ds(k0, k1 - k0)],
                    s2.at[n, d - 1], r2.at[n, d - 1], device_id={"rows": to}, device_id_type=MESH,
                )
                nxt.start()
                copies2[n].append(nxt)

    def start_spans(n):
        k0, k1 = CUTS[n]
        total = wg[row, k0:k1] + got1[0, k0:k1]
        for d, cp in enumerate(copies2[n]):
            cp.wait()
            total = total + got2[d, k0:k1].astype(jnp.float32)
        turned = total.reshape((k1 - k0) * wide, 3 * CH).T
        for t in range(spans):
            for c in range(3):
                piece = turned[c * CH + t * part:c * CH + (t + 1) * part]
                zfull[n][t, c] = piece
                zsend[n][t, c] = piece.astype(jnp.bfloat16)
        copies3[n] = []
        for d in range(1, spans):
            to = lax.rem(span + d, spans)
            cp = pltpu.make_async_remote_copy(
                zsend[n].at[to], got3[n].at[d - 1], s3.at[n, d - 1], r3.at[n, d - 1],
                device_id={"tm": to}, device_id_type=MESH,
            )
            cp.start()
            copies3[n].append(cp)

    def finish(n):
        final = zfull[n][span]
        for d, cp in enumerate(copies3[n]):
            cp.wait()
            final = final + got3[n][d].astype(jnp.float32)
        share[n][...] = final * factor

    step = 26 if cells % 26 == 0 else 2
    steps = cells // step

    def adjoint(j, carry):
        w0 = j * step
        acc = jnp.zeros((step * frames, CH), jnp.float32)
        for k in range(9):
            for c in range(3):
                g = gc[k, pl.ds(w0 + 2 - c, step)].reshape(step * frames, CH)
                acc = acc + lax.dot_general(
                    g, kern_ref[3 * k + c], (((1,), (1,)), ((), ())), preferred_element_type=jnp.float32
                )
        acc = acc.reshape(step, frames, CH)
        xf = xc[pl.ds(w0, step)].astype(jnp.float32)
        s = 1.0 / (1.0 + jnp.exp(-xf))
        res = jnp.where(live[None], acc * (s * (1.0 + xf * (1.0 - s))), 0.0).astype(jnp.bfloat16)
        for p in range(step // 2):
            at = pl.multiple_of((w0 + 2 * p) * CH, 128)
            out_ref[:, pl.ds(at, PAIR)] = jnp.concatenate([res[2 * p], res[2 * p + 1]], axis=1)
        return carry

    lax.fori_loop(*CUTS[0], weight, 0)
    pl.semaphore_wait(barrier, half + spans - 1)
    start_core(0)
    lax.fori_loop(*CUTS[1], weight, 0)
    start_core(1)
    start_rows(0)
    lax.fori_loop(0, steps // 4, adjoint, 0)
    start_rows(1)
    lax.fori_loop(steps // 4, 3 * steps // 4, adjoint, 0)
    start_spans(0)
    lax.fori_loop(3 * steps // 4, steps, adjoint, 0)
    start_spans(1)
    finish(0)
    finish(1)


def body(inputs, cotangent, kernel, span_frames):
    batch, slots, strip, flat = inputs.shape
    cells = flat // CH
    frames = batch * slots
    assert strip == 1 and cells % 2 == 0 and frames % 16 == 0
    spans, strips = lax.axis_size("tm"), lax.axis_size("rows")
    assert strips % 2 == 0 and CH % spans == 0 and CH % strips == 0
    span = lax.axis_index("tm")
    count = jnp.sum(jnp.where(jnp.arange(span_frames.shape[0], dtype=jnp.int32) == span, span_frames, 0))
    x = inputs.reshape(batch, slots, flat).transpose(1, 0, 2).reshape(frames, flat)
    cot = cotangent.reshape(batch, slots, flat).transpose(1, 0, 2)

    back = [(i + 1, i) for i in range(spans - 1)]
    after_one = lax.ppermute(cot[0], "tm", back)
    after_two = lax.ppermute(jnp.where(count >= 2, cot[1], after_one), "tm", back)
    order = jnp.arange(slots + 2, dtype=jnp.int32)[:, None, None]
    ext = jnp.pad(cot, ((0, 2), (0, 0), (0, 0)))
    ext = jnp.where(order < count, ext, jnp.zeros_like(ext))
    ext = jnp.where(order == count, after_one[None], ext)
    ext = jnp.where(order == count + 1, after_two[None], ext)
    ext = ext.reshape(frames + 2 * batch, flat)
    up = [(i, i + 1) for i in range(strips - 1)]
    down = [(i + 1, i) for i in range(strips - 1)]
    above = lax.ppermute(ext, "rows", up)
    below = lax.ppermute(ext, "rows", down)
    live = jnp.arange(frames, dtype=jnp.int32) < count * batch
    mask = jnp.broadcast_to(live[:, None], (frames, CH)).astype(jnp.float32)

    vmem = pl.BlockSpec(memory_space=pltpu.VMEM)
    wide, part, half = CH // strips, CH // spans, strips // 2
    total_cells = batch * slots * spans * strip * strips * cells
    few, some = max(half - 1, 1), max(spans - 1, 1)
    sizes = [k1 - k0 for k0, k1 in CUTS]
    zblocks = [(3, part, n * wide) for n in sizes]
    dma = pltpu.SemaphoreType.DMA
    block = (9, wide, 3 * CH)
    grad_in, *shares = pl.pallas_call(
        functools.partial(kernel_body, cells, strips, spans, float(total_cells) ** -0.5),
        out_shape=(
            jax.ShapeDtypeStruct((frames, flat), jnp.bfloat16),
            jax.ShapeDtypeStruct(zblocks[0], jnp.float32),
            jax.ShapeDtypeStruct(zblocks[1], jnp.float32),
        ),
        in_specs=[vmem] * 6,
        out_specs=(vmem, vmem, vmem),
        scratch_shapes=[
            pltpu.VMEM((cells, frames, CH), jnp.bfloat16),
            pltpu.VMEM((cells + 2, frames, CH), jnp.bfloat16),
            pltpu.VMEM((cells, frames, 3 * CH), jnp.bfloat16),
            pltpu.VMEM((9, cells + 2, frames, CH), jnp.bfloat16),
            pltpu.VMEM((strips,) + block, jnp.float32),
            pltpu.VMEM((half,) + block, jnp.float32),
            pltpu.VMEM((few,) + block, jnp.bfloat16),
            pltpu.VMEM((few,) + block, jnp.bfloat16),
            pltpu.VMEM((spans,) + zblocks[0], jnp.float32),
            pltpu.VMEM((spans,) + zblocks[1], jnp.float32),
            pltpu.VMEM((spans,) + zblocks[0], jnp.bfloat16),
            pltpu.VMEM((spans,) + zblocks[1], jnp.bfloat16),
            pltpu.VMEM((some,) + zblocks[0], jnp.bfloat16),
            pltpu.VMEM((some,) + zblocks[1], jnp.bfloat16),
            dma((2, half)), dma((2, half)), dma((2, few)), dma((2, few)), dma((2, some)), dma((2, some)),
        ],
        compiler_params=pltpu.CompilerParams(
            vmem_limit_bytes=56 << 20, collective_id=0, has_side_effects=True
        ),
        name="fused",
    )(x, mask, below, ext, above, kernel)
    share = jnp.concatenate([s.reshape(3, part, n, wide) for s, n in zip(shares, sizes)], axis=2)
    share = share.transpose(2, 0, 1, 3).reshape(27, part, wide)
    grad_in = grad_in.reshape(slots, batch, strip, flat).transpose(1, 0, 2, 3)
    return grad_in, share


def solution(mesh):
    return jax.shard_map(
        body,
        mesh=mesh,
        in_specs=(
            P("groups", "tm", "rows", None),
            P("groups", "tm", "rows", None),
            P(),
            P("groups"),
        ),
        out_specs=(P("groups", "tm", "rows", None), P("groups", "tm", "rows")),
        check_vma=False,
    )
```

time: 135 us -> 87.9 us (0.65)
  local copies, waits for them, and re-layouts: 46.6 us -> 8.63 us
  Pallas kernels: 66.8 us -> 55.8 us
  waiting for transfers between devices: 8.37 us -> 12.3 us
  starting transfers between devices: 6.96 us -> 5.23 us
    slice x12 -> x0, local copies, waits for them, and re-layouts: 16.6 us -> none  [body(): rows[b][:, 2 - a:2 - a + slots].reshape(frames, flat)]
    another operation x11 -> x0, local copies, waits for them, and re-layouts: 15.8 us -> none  [the longest x10 14.5 us: body(): jnp.stack([rows[b][:, 2 - a:2 - a + slots].reshape(frames, flat) for a in...]
    pallas_call x2 -> x1, Pallas kernels: 66.8 us -> 55.8 us  [body(): pl.pallas_call(functools.partial(kernel_body, cells, strips, spans, float...]
    unnamed x21 -> x11, local copies, waits for them, and re-layouts: 11.7 us -> 1.52 us
    reshape x1 -> x5, local copies, waits for them, and re-layouts: 0.98 us -> 3.71 us  [the longest x2 2.35 us: body(): grad_in = grad_in.reshape(slots, batch, strip, flat).transpose(1, 0, 2, 3)]
    ppermute x2, waiting for transfers between devices: 8.36 us -> 10.4 us  [the longest x1 5.22 us: body(): lax.ppermute(jnp.where(count >= 2, cot[1], after_one), 'tm', back)]
    ppermute x1, waiting for transfers between devices: 0.01 us -> 1.95 us  [body(): below = lax.ppermute(ext, 'rows', down)]
    ppermute x1, starting transfers between devices: 3.08 us -> 1.35 us  [body(): above = lax.ppermute(ext, 'rows', up)]
  transfers between devices with their start and end apart: 4 -> 4, of which waited for: 2 -> 3; matrix products, arithmetic and copies ran while one was open for 16% -> 5% of each run, Pallas kernels for 0% -> 0%
where the time goes in v2:
time: 87.9 us; the launch traced here: 87.5 us
  Pallas kernels  55.8 us (63%)
  waiting for transfers between devices  12.3 us (14%)
  local copies, waits for them, and re-layouts  8.63 us (10%)
  starting transfers between devices  5.23 us (6%)
  other arithmetic  2.88 us (3%)
  between operations  2.72 us (3%)
    pallas_call x1, Pallas kernels, body(): pl.pallas_call(functools.partial(kernel_body, cells, strips, spans, float...  55.8 us
    ppermute x1, waiting for transfers between devices, body(): lax.ppermute(jnp.where(count >= 2, cot[1], after_one), 'tm', back)  5.22 us
    ppermute x1, waiting for transfers between devices, body(): after_one = lax.ppermute(cot[0], 'tm', back)  5.14 us
    reshape x2, local copies, waits for them, and re-layouts, body(): grad_in = grad_in.reshape(slots, batch, strip, flat).transpose(1, 0, 2, 3)  2.35 us
    ppermute x1, waiting for transfers between devices, body(): below = lax.ppermute(ext, 'rows', down)  1.95 us
  transfers between devices with their start and end apart: 4, of which 3 were waited for; matrix products, arithmetic and copies ran while one was open for 5% of the time, Pallas kernels for 0%

profile of v2, /device:TPU:0, one launch (start us, length us, event | category | flops | bytes accessed | tf_op | source)
XLA Modules:
  0.0 87.5 jit_solution(5933043249102499382)
XLA Ops:
  0.6 1.3 %copy.26 = bf16[4,4,1,19968]{3,0,1,2:T(4,128)(2,1)S(1)} copy(bf16[4,4,1,19968]{3,1,2,0:T(4,128)(2,1)} %param.5) | data formatting | bytes 1277952 | tf_op args[1]
  2.0 0.1 slice_bitcast_fusion
  2.0 1.3 %collective-permute-start = (bf16[4,19968]{1,0:T(4,128)(2,1)S(1)}, bf16[4,19968]{1,0:T(4,128)(2,1)S(1)}, u32[]{:S(2)}, u32[]{:S(2)}) collective-permute-start(bf16[4,19968]{1,0:T(4,128)(2,1)S(1)} %slice_bitcast_fusion), channel_id=1, source_target_pairs={{4,0},{8,4},{12,8},{5,1},{9,5},{13,9},{6,2},{10,6},{14,10},{7,3},{... | collective-permute-start | bytes 479240 | tf_op jit(solution)/shard_map/ppermute | solution.py:192
  3.3 1.3 %fusion.1 = s32[]{:T(128)} fusion(s32[4]{0:T(128)} %param.7, s32[]{:T(128)S(6)} %axis_index.15), kind=kLoop, calls=%fused_computation.9 | loop fusion | flops 11 | bytes 24 | tf_op jit(solution)/shard_map/reduce_sum | solution.py:187
  5.9 5.1 %collective-permute-done = bf16[4,19968]{1,0:T(4,128)(2,1)S(1)} collective-permute-done((bf16[4,19968]{1,0:T(4,128)(2,1)S(1)}, bf16[4,19968]{1,0:T(4,128)(2,1)S(1)}, u32[]{:S(2)}, u32[]{:S(2)}) %collective-permute-start) | collective-permute-done | bytes 159776 | tf_op jit(solution)/shard_map/ppermute | solution.py:192
  11.1 0.1 fusion
  11.2 1.3 %collective-permute-start.1 = (bf16[4,19968]{1,0:T(4,128)(2,1)S(1)}, bf16[4,19968]{1,0:T(4,128)(2,1)S(1)}, u32[]{:S(2)}, u32[]{:S(2)}) collective-permute-start(bf16[4,19968]{1,0:T(4,128)(2,1)S(1)} %fusion), channel_id=1, source_target_pairs={{4,0},{8,4},{12,8},{5,1},{9,5},{13,9},{6,2},{10,6},{14,10},{7,3},{... | collective-permute-start | bytes 479240 | tf_op jit(solution)/shard_map/ppermute | solution.py:193
  12.5 0.7 iota_compare_fusion
  13.1 5.2 %collective-permute-done.1 = bf16[4,19968]{1,0:T(4,128)(2,1)S(1)} collective-permute-done((bf16[4,19968]{1,0:T(4,128)(2,1)S(1)}, bf16[4,19968]{1,0:T(4,128)(2,1)S(1)}, u32[]{:S(2)}, u32[]{:S(2)}) %collective-permute-start.1) | collective-permute-done | bytes 159776 | tf_op jit(solution)/shard_map/ppermute | solution.py:193
  18.3 0.8 select_select_fusion
  19.1 0.2 reshape.52.own_ref
  19.4 0.0 copy-start
  19.4 1.4 %collective-permute-start.3 = (bf16[24,19968]{1,0:T(8,128)(2,1)S(1)}, bf16[24,19968]{1,0:T(8,128)(2,1)S(1)}, u32[]{:S(2)}, u32[]{:S(2)}) collective-permute-start(bf16[24,19968]{1,0:T(8,128)(2,1)S(1)} %reshape.52.own_ref), channel_id=1, source_target_pairs={{0,1},{1,2},{2,3},{4,5},{5,6},{6,7},{8,9},{9,10},{10,11},{12,13},{... | collective-permute-start | bytes 2875400 | tf_op jit(solution)/shard_map/ppermute | solution.py:202
  20.7 1.3 %collective-permute-start.2 = (bf16[24,19968]{1,0:T(8,128)(2,1)S(1)}, bf16[24,19968]{1,0:T(8,128)(2,1)S(1)}, u32[]{:S(2)}, u32[]{:S(2)}) collective-permute-start(bf16[24,19968]{1,0:T(8,128)(2,1)S(1)} %reshape.52.own_ref), channel_id=1, source_target_pairs={{1,0},{2,1},{3,2},{5,4},{6,5},{7,6},{9,8},{10,9},{11,10},{13,12},{... | collective-permute-start | bytes 2875400 | tf_op jit(solution)/shard_map/ppermute | solution.py:203
  22.7 1.3 %copy.16 = bf16[4,4,19968]{2,1,0:T(4,128)(2,1)S(1)} copy(bf16[4,4,19968]{2,0,1:T(4,128)(2,1)} %bitcast.28) | data formatting | bytes 1277952 | tf_op jit(solution)/shard_map/transpose | solution.py:188
  24.0 1.0 %reshape.50.x_ref = bf16[16,19968]{1,0:T(8,128)(2,1)} reshape(bf16[4,4,19968]{2,1,0:T(4,128)(2,1)S(1)} %copy.16) | data formatting | bytes 1277952 | tf_op jit(solution)/shard_map/reshape | solution.py:188
  25.0 0.0 collective-permute-done.3.above_ref
  25.0 0.0 copy-start.1
  25.0 1.9 %collective-permute-done.2.below_ref = bf16[24,19968]{1,0:T(8,128)(2,1)S(1)} collective-permute-done((bf16[24,19968]{1,0:T(8,128)(2,1)S(1)}, bf16[24,19968]{1,0:T(8,128)(2,1)S(1)}, u32[]{:S(2)}, u32[]{:S(2)}) %collective-permute-start.2) | collective-permute-done | bytes 958496 | tf_op jit(solution)/shard_map/ppermute | solution.py:203
  27.0 0.0 copy-start.2
  27.0 0.8 broadcast_in_dim.51.mask_ref
  27.7 0.0 copy-done
  27.7 0.0 copy-done.1
  27.7 0.2 copy-done.2
  27.9 55.8 %fused.1 = (bf16[16,19968]{1,0:T(8,128)(2,1)}, f32[3,48,240]{2,1,0:T(8,128)}, f32[3,48,192]{2,1,0:T(8,128)}) custom-call(bf16[16,19968]{1,0:T(8,128)(2,1)} %reshape.50.x_ref, f32[16,192]{1,0:T(8,128)} %broadcast_in_dim.51.mask_ref, bf16[24,19968]{1,0:T(8,128)(2,1)} %copy-done.2, bf16[24,19968]{1,0:T(8,128)(2,1)} %copy-done, bf16[24,19968]{1,0:T(8,128)(2,1)} %copy-done.1, ...), custom_call_target="tpu_custom_call" | custom-call | tf_op jit(solution)/shard_map/fused/pallas_call | solution.py:215
  83.7 0.0 copy-start.3
  83.7 0.0 copy-start.4
  83.7 1.3 %reshape.53 = bf16[4,4,1,19968]{3,1,0,2:T(4,128)(2,1)S(1)} reshape(bf16[16,19968]{1,0:T(8,128)(2,1)} %get-tuple-element.5) | data formatting | bytes 1277952 | tf_op jit(solution)/shard_map/reshape | solution.py:248
  85.0 1.1 %copy.25 = bf16[4,4,1,19968]{3,0,2,1:T(4,128)(2,1)} copy(bf16[4,4,1,19968]{3,1,0,2:T(4,128)(2,1)S(1)} %reshape.53) | data formatting | bytes 1277952 | tf_op jit(solution)/shard_map/reshape | solution.py:248
  86.1 0.0 copy-done.3
  86.1 0.1 copy.22
  86.2 0.0 copy-done.4
  86.2 0.2 copy.19
  86.4 1.1 %copy.21 = f32[9,3,48,48]{3,2,1,0:T(8,128)} copy(f32[9,3,48,48]{2,3,0,1:T(8,128)S(1)} %maximum_bitcast_fusion) | data formatting | bytes 497664 | tf_op jit(solution)/shard_map/transpose | solution.py:247
  (3 shorter events, 0.1 us)
Async XLA Ops:
  2.0 9.0 %collective-permute-start = (bf16[4,19968]{1,0:T(4,128)(2,1)S(1)}, bf16[4,19968]{1,0:T(4,128)(2,1)S(1)}, u32[]{:S(2)}, u32[]{:S(2)}) collective-permute-start(bf16[4,19968]{1,0:T(4,128)(2,1)S(1)} %slice_bitcast_fusion), channel_id=1, source_target_pairs={{4,0},{8,4},{12,8},{5,1},{9,5},{13,9},{6,2},{10,6},{14,10},{7,3},{... | collective-permute-start | bytes 479240 | tf_op jit(solution)/shard_map/ppermute | solution.py:192
  11.2 7.2 %collective-permute-start.1 = (bf16[4,19968]{1,0:T(4,128)(2,1)S(1)}, bf16[4,19968]{1,0:T(4,128)(2,1)S(1)}, u32[]{:S(2)}, u32[]{:S(2)}) collective-permute-start(bf16[4,19968]{1,0:T(4,128)(2,1)S(1)} %fusion), channel_id=1, source_target_pairs={{4,0},{8,4},{12,8},{5,1},{9,5},{13,9},{6,2},{10,6},{14,10},{7,3},{... | collective-permute-start | bytes 479240 | tf_op jit(solution)/shard_map/ppermute | solution.py:193
  19.4 8.4 %copy-start = (bf16[24,19968]{1,0:T(8,128)(2,1)}, bf16[24,19968]{1,0:T(8,128)(2,1)S(1)}, u32[]{:S(2)}) copy-start(bf16[24,19968]{1,0:T(8,128)(2,1)S(1)} %reshape.52.own_ref) | copy-start | bytes 2875396
  19.4 5.6 %collective-permute-start.3 = (bf16[24,19968]{1,0:T(8,128)(2,1)S(1)}, bf16[24,19968]{1,0:T(8,128)(2,1)S(1)}, u32[]{:S(2)}, u32[]{:S(2)}) collective-permute-start(bf16[24,19968]{1,0:T(8,128)(2,1)S(1)} %reshape.52.own_ref), channel_id=1, source_target_pairs={{0,1},{1,2},{2,3},{4,5},{5,6},{6,7},{8,9},{9,10},{10,11},{12,13},{... | collective-permute-start | bytes 2875400 | tf_op jit(solution)/shard_map/ppermute | solution.py:202
  20.7 6.2 %collective-permute-start.2 = (bf16[24,19968]{1,0:T(8,128)(2,1)S(1)}, bf16[24,19968]{1,0:T(8,128)(2,1)S(1)}, u32[]{:S(2)}, u32[]{:S(2)}) collective-permute-start(bf16[24,19968]{1,0:T(8,128)(2,1)S(1)} %reshape.52.own_ref), channel_id=1, source_target_pairs={{1,0},{2,1},{3,2},{5,4},{6,5},{7,6},{9,8},{10,9},{11,10},{13,12},{... | collective-permute-start | bytes 2875400 | tf_op jit(solution)/shard_map/ppermute | solution.py:203
  25.0 2.7 %copy-start.1 = (bf16[24,19968]{1,0:T(8,128)(2,1)}, bf16[24,19968]{1,0:T(8,128)(2,1)S(1)}, u32[]{:S(2)}) copy-start(bf16[24,19968]{1,0:T(8,128)(2,1)S(1)} %collective-permute-done.3.above_ref) | copy-start | bytes 2875396
  27.0 0.9 %copy-start.2 = (bf16[24,19968]{1,0:T(8,128)(2,1)}, bf16[24,19968]{1,0:T(8,128)(2,1)S(1)}, u32[]{:S(2)}) copy-start(bf16[24,19968]{1,0:T(8,128)(2,1)S(1)} %collective-permute-done.2.below_ref) | copy-start | bytes 2875396
  83.7 2.4 %copy-start.3 = (f32[3,48,192]{2,1,0:T(8,128)S(1)}, f32[3,48,192]{2,1,0:T(8,128)}, u32[]{:S(2)}) copy-start(f32[3,48,192]{2,1,0:T(8,128)} %get-tuple-element.7) | copy-start | bytes 331780
  83.7 2.5 %copy-start.4 = (f32[3,48,240]{2,1,0:T(8,128)S(1)}, f32[3,48,240]{2,1,0:T(8,128)}, u32[]{:S(2)}) copy-start(f32[3,48,240]{2,1,0:T(8,128)} %get-tuple-element.6) | copy-start | bytes 414724

commit v3 on v2

--- a/solution.py
+++ b/solution.py
@@ -14,9 +14,9 @@
 CUTS = ((0, 5), (5, 9))
 
 
-def kernel_body(cells, strips, spans, factor, x_ref, mask_ref, below_ref, own_ref, above_ref, kern_ref,
+def kernel_body(cells, strips, spans, factor, x_ref, mask_ref, own_ref, kern_ref,
                 out_ref, share0_ref, share1_ref, xc, act, act3, gc, wg, got1, send2, got2,
-                zfull0, zfull1, zsend0, zsend1, got30, got31, s1, r1, s2, r2, s3, r3):
+                zfull0, zfull1, zsend0, zsend1, got30, got31, near, s1, r1, s2, r2, s3, r3, sn, rn):
     frames = x_ref.shape[0]
     tail = own_ref.shape[0] - frames
     batch = tail // 2
@@ -34,14 +34,24 @@
         return lax.rem(place + d, half)
 
     barrier = pltpu.get_barrier_semaphore()
-    pl.semaphore_signal(barrier, inc=1, device_id={"rows": partner}, device_id_type=MESH)
-    for d in range(1, half):
-        pl.semaphore_signal(barrier, inc=1, device_id={"rows": 2 * strip_at(d) + parity}, device_id_type=MESH)
+    for d in range(1, strips):
+        pl.semaphore_signal(barrier, inc=1, device_id={"rows": lax.rem(row + d, strips)}, device_id_type=MESH)
     for d in range(1, spans):
         pl.semaphore_signal(barrier, inc=1, device_id={"tm": lax.rem(span + d, spans)}, device_id_type=MESH)
 
+    pl.semaphore_wait(barrier, strips + spans - 2)
+    has_above, has_below = row > 0, row < strips - 1
+    near_copies = [
+        pltpu.make_async_remote_copy(
+            own_ref, near.at[n], sn.at[n], rn.at[n],
+            device_id={"rows": lax.rem(row + strips + move, strips)}, device_id_type=MESH,
+        )
+        for n, move in enumerate((-1, 1))
+    ]
+    pl.when(has_above)(near_copies[0].start)
+    pl.when(has_below)(near_copies[1].start)
+
     live = mask_ref[...] > 0.5
-    grads = (below_ref, own_ref, above_ref)
 
     def split(p, carry):
         at = pl.multiple_of(p * PAIR, 128)
@@ -52,13 +62,21 @@
             xf = cell.astype(jnp.float32)
             s = 1.0 / (1.0 + jnp.exp(-xf))
             act[2 * p + q + 1] = jnp.where(live, xf * s, 0.0).astype(jnp.bfloat16)
-        for b in range(3):
-            v = grads[b][:, pl.ds(at, PAIR)]
-            for q in range(2):
-                cell = v[:, q * CH:(q + 1) * CH]
-                for a in range(3):
-                    lo = (2 - a) * batch
-                    gc[3 * a + b, 2 * p + q + 1] = cell[lo:lo + frames]
+        return split_row(own_ref, 0, p, carry)
+
+    def split_row(ref, b, p, carry):
+        at = pl.multiple_of(p * PAIR, 128)
+        v = ref[:, pl.ds(at, PAIR)]
+        for q in range(2):
+            cell = v[:, q * CH:(q + 1) * CH]
+            for a in range(3):
+                lo = (2 - a) * batch
+                gc[3 * b + a, 2 * p + q + 1] = cell[lo:lo + frames]
+        return carry
+
+    def split_near(p, carry):
+        for n in range(2):
+            split_row(near.at[n], n + 1, p, carry)
         return carry
 
     zero = jnp.zeros((frames, CH), jnp.bfloat16)
@@ -149,7 +167,7 @@
             for c in range(3):
                 g = gc[k, pl.ds(w0 + 2 - c, step)].reshape(step * frames, CH)
                 acc = acc + lax.dot_general(
-                    g, kern_ref[3 * k + c], (((1,), (1,)), ((), ())), preferred_element_type=jnp.float32
+                    g, kern_ref[9 * (k % 3) + 3 * (1, 0, 2)[k // 3] + c], (((1,), (1,)), ((), ())), preferred_element_type=jnp.float32
                 )
         acc = acc.reshape(step, frames, CH)
         xf = xc[pl.ds(w0, step)].astype(jnp.float32)
@@ -160,8 +178,31 @@
             out_ref[:, pl.ds(at, PAIR)] = jnp.concatenate([res[2 * p], res[2 * p + 1]], axis=1)
         return carry
 
-    lax.fori_loop(*CUTS[0], weight, 0)
-    pl.semaphore_wait(barrier, half + spans - 1)
+    lax.fori_loop(0, 3, weight, 0)
+
+    @pl.when(has_below)
+    def _():
+        near_copies[0].wait_recv()
+
+    @pl.when(has_above)
+    def _():
+        near_copies[0].wait_send()
+        near_copies[1].wait_recv()
+
+    @pl.when(has_below)
+    def _():
+        near_copies[1].wait_send()
+
+    @pl.when(row == strips - 1)
+    def _():
+        near[0] = jnp.zeros(near.shape[1:], near.dtype)
+
+    @pl.when(row == 0)
+    def _():
+        near[1] = jnp.zeros(near.shape[1:], near.dtype)
+
+    lax.fori_loop(0, pairs, split_near, 0)
+    lax.fori_loop(3, CUTS[0][1], weight, 0)
     start_core(0)
     lax.fori_loop(*CUTS[1], weight, 0)
     start_core(1)
@@ -197,10 +238,6 @@
     ext = jnp.where(order == count, after_one[None], ext)
     ext = jnp.where(order == count + 1, after_two[None], ext)
     ext = ext.reshape(frames + 2 * batch, flat)
-    up = [(i, i + 1) for i in range(strips - 1)]
-    down = [(i + 1, i) for i in range(strips - 1)]
-    above = lax.ppermute(ext, "rows", up)
-    below = lax.ppermute(ext, "rows", down)
     live = jnp.arange(frames, dtype=jnp.int32) < count * batch
     mask = jnp.broadcast_to(live[:, None], (frames, CH)).astype(jnp.float32)
 
@@ -219,7 +256,7 @@
             jax.ShapeDtypeStruct(zblocks[0], jnp.float32),
             jax.ShapeDtypeStruct(zblocks[1], jnp.float32),
         ),
-        in_specs=[vmem] * 6,
+        in_specs=[vmem] * 4,
         out_specs=(vmem, vmem, vmem),
         scratch_shapes=[
             pltpu.VMEM((cells, frames, CH), jnp.bfloat16),
@@ -236,15 +273,19 @@
             pltpu.VMEM((spans,) + zblocks[1], jnp.bfloat16),
             pltpu.VMEM((some,) + zblocks[0], jnp.bfloat16),
             pltpu.VMEM((some,) + zblocks[1], jnp.bfloat16),
+            pltpu.VMEM((2, frames + 2 * batch, flat), jnp.bfloat16),
             dma((2, half)), dma((2, half)), dma((2, few)), dma((2, few)), dma((2, some)), dma((2, some)),
+            dma((2,)), dma((2,)),
         ],
         compiler_params=pltpu.CompilerParams(
             vmem_limit_bytes=56 << 20, collective_id=0, has_side_effects=True
         ),
         name="fused",
-    )(x, mask, below, ext, above, kernel)
+    )(x, mask, ext, kernel)
     share = jnp.concatenate([s.reshape(3, part, n, wide) for s, n in zip(shares, sizes)], axis=2)
-    share = share.transpose(2, 0, 1, 3).reshape(27, part, wide)
+    share = share.reshape(3, part, 3, 3, wide)
+    share = jnp.concatenate([share[:, :, 1:2], share[:, :, 0:1], share[:, :, 2:3]], axis=2)
+    share = share.transpose(3, 2, 0, 1, 4).reshape(27, part, wide)
     grad_in = grad_in.reshape(slots, batch, strip, flat).transpose(1, 0, 2, 3)
     return grad_in, share
 

time: 87.9 us -> 76.2 us (0.87)
  Pallas kernels: 55.8 us -> 50.2 us
  waiting for transfers between devices: 12.3 us -> 7.38 us
  starting transfers between devices: 5.23 us -> 2.58 us
  local copies, waits for them, and re-layouts: 8.63 us -> 10.1 us
    pallas_call x1, Pallas kernels: 55.8 us -> 50.2 us  [body(): pl.pallas_call(functools.partial(kernel_body, cells, strips, spans, float...]
    ppermute x2 -> x0, starting transfers between devices: 2.64 us -> none  [the longest x1 1.35 us: body(): above = lax.ppermute(ext, 'rows', up)]
    ppermute x1, waiting for transfers between devices: 5.22 us -> 2.9 us  [body(): lax.ppermute(jnp.where(count >= 2, cot[1], after_one), 'tm', back)]
    ppermute x2 -> x0, waiting for transfers between devices: 1.95 us -> none  [the longest x1 1.95 us: body(): below = lax.ppermute(ext, 'rows', down)]
    reshape x2, local copies, waits for them, and re-layouts: 2.35 us -> 1.22 us  [body(): grad_in = grad_in.reshape(slots, batch, strip, flat).transpose(1, 0, 2, 3)]
    reshape x1, local copies, waits for them, and re-layouts: 0.23 us -> 1.18 us  [body(): ext = ext.reshape(frames + 2 * batch, flat)]
    reshape x1, local copies, waits for them, and re-layouts: 0.15 us -> 1.06 us  [body(): s.reshape(3, part, n, wide)]
    pallas_call x1, local copies, waits for them, and re-layouts: 0.16 us -> 1.07 us  [body(): pl.pallas_call(functools.partial(kernel_body, cells, strips, spans, float...]
  transfers between devices with their start and end apart: 4 -> 2, of which waited for: 3 -> 2; matrix products, arithmetic and copies ran while one was open for 5% -> 6% of each run, Pallas kernels for 0% -> 0%
where the time goes in v3:
time: 76.2 us; the launch traced here: 75.9 us
  Pallas kernels  50.2 us (66%)
  local copies, waits for them, and re-layouts  10.1 us (13%)
  waiting for transfers between devices  7.38 us (10%)
  other arithmetic  2.95 us (4%)
  between operations  2.69 us (4%)
  starting transfers between devices  2.58 us (3%)
    pallas_call x1, Pallas kernels, body(): pl.pallas_call(functools.partial(kernel_body, cells, strips, spans, float...  50.2 us
    ppermute x1, waiting for transfers between devices, body(): after_one = lax.ppermute(cot[0], 'tm', back)  4.48 us
    ppermute x1, waiting for transfers between devices, body(): lax.ppermute(jnp.where(count >= 2, cot[1], after_one), 'tm', back)  2.9 us
  transfers between devices with their start and end apart: 2, of which 2 were waited for; matrix products, arithmetic and copies ran while one was open for 6% of the time, Pallas kernels for 0%

profile of v3, /device:TPU:0, one launch (start us, length us, event | category | flops | bytes accessed | tf_op | source)
XLA Modules:
  0.0 75.9 jit_solution(17745814174704782116)
XLA Ops:
  0.6 1.3 %copy.30 = bf16[4,4,1,19968]{3,0,1,2:T(4,128)(2,1)S(1)} copy(bf16[4,4,1,19968]{3,1,2,0:T(4,128)(2,1)} %param.5) | data formatting | bytes 1277952 | tf_op args[1]
  2.0 0.1 slice_bitcast_fusion
  2.0 1.3 %collective-permute-start = (bf16[4,19968]{1,0:T(4,128)(2,1)S(1)}, bf16[4,19968]{1,0:T(4,128)(2,1)S(1)}, u32[]{:S(2)}, u32[]{:S(2)}) collective-permute-start(bf16[4,19968]{1,0:T(4,128)(2,1)S(1)} %slice_bitcast_fusion), channel_id=1, source_target_pairs={{4,0},{8,4},{12,8},{5,1},{9,5},{13,9},{6,2},{10,6},{14,10},{7,3},{... | collective-permute-start | bytes 479240 | tf_op jit(solution)/shard_map/ppermute | solution.py:233
  3.3 1.3 %fusion.1 = s32[]{:T(128)} fusion(s32[4]{0:T(128)} %param.7, s32[]{:T(128)S(6)} %axis_index.15), kind=kLoop, calls=%fused_computation.10 | loop fusion | flops 11 | bytes 24 | tf_op jit(solution)/shard_map/reduce_sum | solution.py:228
  6.6 4.5 %collective-permute-done = bf16[4,19968]{1,0:T(4,128)(2,1)S(1)} collective-permute-done((bf16[4,19968]{1,0:T(4,128)(2,1)S(1)}, bf16[4,19968]{1,0:T(4,128)(2,1)S(1)}, u32[]{:S(2)}, u32[]{:S(2)}) %collective-permute-start) | collective-permute-done | bytes 159776 | tf_op jit(solution)/shard_map/ppermute | solution.py:233
  11.1 0.1 fusion
  11.2 1.3 %collective-permute-start.1 = (bf16[4,19968]{1,0:T(4,128)(2,1)S(1)}, bf16[4,19968]{1,0:T(4,128)(2,1)S(1)}, u32[]{:S(2)}, u32[]{:S(2)}) collective-permute-start(bf16[4,19968]{1,0:T(4,128)(2,1)S(1)} %fusion), channel_id=1, source_target_pairs={{4,0},{8,4},{12,8},{5,1},{9,5},{13,9},{6,2},{10,6},{14,10},{7,3},{... | collective-permute-start | bytes 479240 | tf_op jit(solution)/shard_map/ppermute | solution.py:234
  12.5 1.3 %copy.19 = bf16[4,4,19968]{2,1,0:T(4,128)(2,1)S(1)} copy(bf16[4,4,19968]{2,0,1:T(4,128)(2,1)} %bitcast.30) | data formatting | bytes 1277952 | tf_op jit(solution)/shard_map/transpose | solution.py:229
  13.8 1.0 %reshape.53.x_ref = bf16[16,19968]{1,0:T(8,128)(2,1)} reshape(bf16[4,4,19968]{2,1,0:T(4,128)(2,1)S(1)} %copy.19) | data formatting | bytes 1277952 | tf_op jit(solution)/shard_map/reshape | solution.py:229
  14.8 0.6 iota_compare_fusion
  15.4 2.9 %collective-permute-done.1 = bf16[4,19968]{1,0:T(4,128)(2,1)S(1)} collective-permute-done((bf16[4,19968]{1,0:T(4,128)(2,1)S(1)}, bf16[4,19968]{1,0:T(4,128)(2,1)S(1)}, u32[]{:S(2)}, u32[]{:S(2)}) %collective-permute-start.1) | collective-permute-done | bytes 159776 | tf_op jit(solution)/shard_map/ppermute | solution.py:234
  18.3 0.8 %select_select_fusion = bf16[6,4,19968]{2,1,0:T(4,128)(2,1)S(1)} fusion(bf16[4,4,19968]{2,1,0:T(4,128)(2,1)S(1)} %bitcast.25, pred[6]{0:T(512)(128)(4,1)S(1)} %get-tuple-element.11, pred[6]{0:T(512)(128)(4,1)S(1)} %get-tuple-element.12, pred[6]{0:T(512)(128)(4,1)S(1)} %iota_compare_fusion.2, bf16[4,19968]{1,0:T(4,128)(2,1)S(1)} %collective-permute-done, ...), kind=kLoop, calls=%fused_computation | loop fusion | flops 1437696 | bytes 1916946 | tf_op jit(solution)/shard_map/jit(_where)/select_n | solution.py:239
  19.1 1.2 %reshape.55.own_ref = bf16[24,19968]{1,0:T(8,128)(2,1)} reshape(bf16[6,4,19968]{2,1,0:T(4,128)(2,1)S(1)} %select_select_fusion) | data formatting | bytes 1916928 | tf_op jit(solution)/shard_map/reshape | solution.py:240
  20.3 0.7 broadcast_in_dim.51.mask_ref
  21.0 50.2 %fused.1 = (bf16[16,19968]{1,0:T(8,128)(2,1)}, f32[3,48,240]{2,1,0:T(8,128)}, f32[3,48,192]{2,1,0:T(8,128)}) custom-call(bf16[16,19968]{1,0:T(8,128)(2,1)} %reshape.53.x_ref, f32[16,192]{1,0:T(8,128)} %broadcast_in_dim.51.mask_ref, bf16[24,19968]{1,0:T(8,128)(2,1)} %reshape.55.own_ref, bf16[27,192,192]{2,1,0:T(8,128)(2,1)} %kern_ref.1), custom_call_target="tpu_custom_call" | custom-call | tf_op jit(solution)/shard_map/fused/pallas_call | solution.py:252
  71.2 1.1 %copy.22 = f32[3,48,240]{1,2,0:T(8,128)S(1)} copy(f32[3,48,240]{2,1,0:T(8,128)} %get-tuple-element.6) | data formatting | bytes 276480 | tf_op jit(solution)/shard_map/fused/pallas_call | solution.py:252
  72.3 1.1 %copy.26 = f32[3,48,192]{1,2,0:T(8,128)S(1)} copy(f32[3,48,192]{2,1,0:T(8,128)} %get-tuple-element.7) | data formatting | bytes 221184 | tf_op jit(solution)/shard_map/reshape | solution.py:285
  73.4 0.0 copy-start
  73.4 0.2 copy.24
  73.7 0.1 maximum_bitcast_fusion
  73.8 0.9 %copy.25 = f32[3,3,3,48,48]{4,3,2,1,0:T(8,128)} copy(f32[3,3,3,48,48]{4,3,0,1,2:T(8,128)S(1)} %maximum_bitcast_fusion) | data formatting | bytes 497664 | tf_op jit(solution)/shard_map/transpose | solution.py:288
  74.6 0.0 copy-done
  74.6 0.1 reshape.56
  74.8 1.1 %copy.29 = bf16[4,4,1,19968]{3,0,2,1:T(4,128)(2,1)} copy(bf16[4,4,1,19968]{3,1,0,2:T(4,128)(2,1)S(1)} %reshape.56) | data formatting | bytes 1277952 | tf_op jit(solution)/shard_map/reshape | solution.py:289
  (4 shorter events, 0.1 us)
Async XLA Ops:
  2.0 9.0 %collective-permute-start = (bf16[4,19968]{1,0:T(4,128)(2,1)S(1)}, bf16[4,19968]{1,0:T(4,128)(2,1)S(1)}, u32[]{:S(2)}, u32[]{:S(2)}) collective-permute-start(bf16[4,19968]{1,0:T(4,128)(2,1)S(1)} %slice_bitcast_fusion), channel_id=1, source_target_pairs={{4,0},{8,4},{12,8},{5,1},{9,5},{13,9},{6,2},{10,6},{14,10},{7,3},{... | collective-permute-start | bytes 479240 | tf_op jit(solution)/shard_map/ppermute | solution.py:233
  11.2 7.2 %collective-permute-start.1 = (bf16[4,19968]{1,0:T(4,128)(2,1)S(1)}, bf16[4,19968]{1,0:T(4,128)(2,1)S(1)}, u32[]{:S(2)}, u32[]{:S(2)}) collective-permute-start(bf16[4,19968]{1,0:T(4,128)(2,1)S(1)} %fusion), channel_id=1, source_target_pairs={{4,0},{8,4},{12,8},{5,1},{9,5},{13,9},{6,2},{10,6},{14,10},{7,3},{... | collective-permute-start | bytes 479240 | tf_op jit(solution)/shard_map/ppermute | solution.py:234
  73.4 1.3 %copy-start = (bf16[16,19968]{1,0:T(8,128)(2,1)S(1)}, bf16[16,19968]{1,0:T(8,128)(2,1)}, u32[]{:S(2)}) copy-start(bf16[16,19968]{1,0:T(8,128)(2,1)} %get-tuple-element.5) | copy-start | bytes 1916932

commit v4 on v3

--- a/solution.py
+++ b/solution.py
@@ -11,18 +11,17 @@
 PAIR = 2 * CH
 MESH = pl.DeviceIdType.MESH
 
-CUTS = ((0, 5), (5, 9))
+CUTS = ((0, 3), (3, 6), (6, 9))
 
 
 def kernel_body(cells, strips, spans, factor, x_ref, mask_ref, own_ref, kern_ref,
-                out_ref, share0_ref, share1_ref, xc, act, act3, gc, wg, got1, send2, got2,
-                zfull0, zfull1, zsend0, zsend1, got30, got31, near, s1, r1, s2, r2, s3, r3, sn, rn):
+                out_ref, share_ref, xc, act, act3, gc, wg, got1, send2, got2,
+                zfull, zsend, got3, near, s1, r1, s2, r2, s3, r3, sn, rn):
     frames = x_ref.shape[0]
     tail = own_ref.shape[0] - frames
     batch = tail // 2
     pairs = cells // 2
     wide, part, half = CH // strips, CH // spans, strips // 2
-    share, zfull, zsend, got3 = (share0_ref, share1_ref), (zfull0, zfull1), (zsend0, zsend1), (got30, got31)
     row = lax.axis_index("rows")
     span = lax.axis_index("tm")
     place = row // 2
@@ -136,26 +135,27 @@
             total = total + got2[d, k0:k1].astype(jnp.float32)
         turned = total.reshape((k1 - k0) * wide, 3 * CH).T
         for t in range(spans):
-            for c in range(3):
-                piece = turned[c * CH + t * part:c * CH + (t + 1) * part]
-                zfull[n][t, c] = piece
-                zsend[n][t, c] = piece.astype(jnp.bfloat16)
+            piece = jnp.concatenate(
+                [turned[c * CH + t * part:c * CH + (t + 1) * part] for c in range(3)], axis=1
+            )
+            zfull[n, t] = piece
+            zsend[n, t] = piece.astype(jnp.bfloat16)
         copies3[n] = []
         for d in range(1, spans):
             to = lax.rem(span + d, spans)
             cp = pltpu.make_async_remote_copy(
-                zsend[n].at[to], got3[n].at[d - 1], s3.at[n, d - 1], r3.at[n, d - 1],
+                zsend.at[n, to], got3.at[n, d - 1], s3.at[n, d - 1], r3.at[n, d - 1],
                 device_id={"tm": to}, device_id_type=MESH,
             )
             cp.start()
             copies3[n].append(cp)
 
     def finish(n):
-        final = zfull[n][span]
+        final = zfull[n, span]
         for d, cp in enumerate(copies3[n]):
             cp.wait()
-            final = final + got3[n][d].astype(jnp.float32)
-        share[n][...] = final * factor
+            final = final + got3[n, d].astype(jnp.float32)
+        share_ref[n] = final * factor
 
     step = 26 if cells % 26 == 0 else 2
     steps = cells // step
@@ -178,7 +178,9 @@
             out_ref[:, pl.ds(at, PAIR)] = jnp.concatenate([res[2 * p], res[2 * p + 1]], axis=1)
         return carry
 
-    lax.fori_loop(0, 3, weight, 0)
+    lax.fori_loop(*CUTS[0], weight, 0)
+    start_core(0)
+    start_rows(0)
 
     @pl.when(has_below)
     def _():
@@ -202,19 +204,20 @@
         near[1] = jnp.zeros(near.shape[1:], near.dtype)
 
     lax.fori_loop(0, pairs, split_near, 0)
-    lax.fori_loop(3, CUTS[0][1], weight, 0)
-    start_core(0)
     lax.fori_loop(*CUTS[1], weight, 0)
     start_core(1)
-    start_rows(0)
+    start_spans(0)
+    lax.fori_loop(*CUTS[2], weight, 0)
+    start_core(2)
+    start_rows(1)
     lax.fori_loop(0, steps // 4, adjoint, 0)
-    start_rows(1)
+    start_rows(2)
     lax.fori_loop(steps // 4, 3 * steps // 4, adjoint, 0)
-    start_spans(0)
+    start_spans(1)
     lax.fori_loop(3 * steps // 4, steps, adjoint, 0)
-    start_spans(1)
-    finish(0)
-    finish(1)
+    start_spans(2)
+    for n in range(3):
+        finish(n)
 
 
 def body(inputs, cotangent, kernel, span_frames):
@@ -245,19 +248,17 @@
     wide, part, half = CH // strips, CH // spans, strips // 2
     total_cells = batch * slots * spans * strip * strips * cells
     few, some = max(half - 1, 1), max(spans - 1, 1)
-    sizes = [k1 - k0 for k0, k1 in CUTS]
-    zblocks = [(3, part, n * wide) for n in sizes]
+    zblock = (part, 9 * wide)
     dma = pltpu.SemaphoreType.DMA
     block = (9, wide, 3 * CH)
-    grad_in, *shares = pl.pallas_call(
+    grad_in, share = pl.pallas_call(
         functools.partial(kernel_body, cells, strips, spans, float(total_cells) ** -0.5),
         out_shape=(
             jax.ShapeDtypeStruct((frames, flat), jnp.bfloat16),
-            jax.ShapeDtypeStruct(zblocks[0], jnp.float32),
-            jax.ShapeDtypeStruct(zblocks[1], jnp.float32),
+            jax.ShapeDtypeStruct((3,) + zblock, jnp.float32),
         ),
         in_specs=[vmem] * 4,
-        out_specs=(vmem, vmem, vmem),
+        out_specs=(vmem, vmem),
         scratch_shapes=[
             pltpu.VMEM((cells, frames, CH), jnp.bfloat16),
             pltpu.VMEM((cells + 2, frames, CH), jnp.bfloat16),
@@ -267,14 +268,11 @@
             pltpu.VMEM((half,) + block, jnp.float32),
             pltpu.VMEM((few,) + block, jnp.bfloat16),
             pltpu.VMEM((few,) + block, jnp.bfloat16),
-            pltpu.VMEM((spans,) + zblocks[0], jnp.float32),
-            pltpu.VMEM((spans,) + zblocks[1], jnp.float32),
-            pltpu.VMEM((spans,) + zblocks[0], jnp.bfloat16),
-            pltpu.VMEM((spans,) + zblocks[1], jnp.bfloat16),
-            pltpu.VMEM((some,) + zblocks[0], jnp.bfloat16),
-            pltpu.VMEM((some,) + zblocks[1], jnp.bfloat16),
+            pltpu.VMEM((3, spans) + zblock, jnp.float32),
+            pltpu.VMEM((3, spans) + zblock, jnp.bfloat16),
+            pltpu.VMEM((3, some) + zblock, jnp.bfloat16),
             pltpu.VMEM((2, frames + 2 * batch, flat), jnp.bfloat16),
-            dma((2, half)), dma((2, half)), dma((2, few)), dma((2, few)), dma((2, some)), dma((2, some)),
+            dma((3, half)), dma((3, half)), dma((3, few)), dma((3, few)), dma((3, some)), dma((3, some)),
             dma((2,)), dma((2,)),
         ],
         compiler_params=pltpu.CompilerParams(
@@ -282,10 +280,9 @@
         ),
         name="fused",
     )(x, mask, ext, kernel)
-    share = jnp.concatenate([s.reshape(3, part, n, wide) for s, n in zip(shares, sizes)], axis=2)
     share = share.reshape(3, part, 3, 3, wide)
-    share = jnp.concatenate([share[:, :, 1:2], share[:, :, 0:1], share[:, :, 2:3]], axis=2)
-    share = share.transpose(3, 2, 0, 1, 4).reshape(27, part, wide)
+    share = jnp.stack([share[1], share[0], share[2]])
+    share = share.transpose(3, 0, 2, 1, 4).reshape(27, part, wide)
     grad_in = grad_in.reshape(slots, batch, strip, flat).transpose(1, 0, 2, 3)
     return grad_in, share
 

time: 76.2 us -> 73.6 us (0.966)
  Pallas kernels: 50.2 us -> 48.2 us
  local copies, waits for them, and re-layouts: 10.1 us -> 9.27 us
    pallas_call x1, Pallas kernels: 50.2 us -> 48.2 us  [body(): pl.pallas_call(functools.partial(kernel_body, cells, strips, spans, float...]
    slice x1 -> x4, local copies, waits for them, and re-layouts: 0.05 us -> 1.6 us  [body(): share = jnp.stack([share[1], share[0], share[2]])]
    pallas_call x1 -> x0, local copies, waits for them, and re-layouts: 1.07 us -> none  [body(): pl.pallas_call(functools.partial(kernel_body, cells, strips, spans, float...]
    reshape x1 -> x0, local copies, waits for them, and re-layouts: 1.06 us -> none  [body(): s.reshape(3, part, n, wide)]
where the time goes in v4:
time: 73.6 us; the launch traced here: 73.2 us
  Pallas kernels  48.2 us (65%)
  local copies, waits for them, and re-layouts  9.27 us (13%)
  waiting for transfers between devices  7.38 us (10%)
  other arithmetic  3.06 us (4%)
  between operations  2.7 us (4%)
  starting transfers between devices  2.58 us (4%)
    pallas_call x1, Pallas kernels, body(): pl.pallas_call(functools.partial(kernel_body, cells, strips, spans, float...  48.2 us
    ppermute x1, waiting for transfers between devices, body(): after_one = lax.ppermute(cot[0], 'tm', back)  4.48 us
    ppermute x1, waiting for transfers between devices, body(): lax.ppermute(jnp.where(count >= 2, cot[1], after_one), 'tm', back)  2.9 us
    slice x4, local copies, waits for them, and re-layouts, body(): share = jnp.stack([share[1], share[0], share[2]])  1.6 us
  transfers between devices with their start and end apart: 2, of which 2 were waited for; matrix products, arithmetic and copies ran while one was open for 6% of the time, Pallas kernels for 0%

profile of v4, /device:TPU:0, one launch (start us, length us, event | category | flops | bytes accessed | tf_op | source)
XLA Modules:
  0.0 73.2 jit_solution(9007178269745742543)
XLA Ops:
  0.6 1.3 %copy.21 = bf16[4,4,1,19968]{3,0,1,2:T(4,128)(2,1)S(1)} copy(bf16[4,4,1,19968]{3,1,2,0:T(4,128)(2,1)} %param.5) | data formatting | bytes 1277952 | tf_op args[1]
  2.0 0.1 slice_bitcast_fusion
  2.0 1.3 %collective-permute-start = (bf16[4,19968]{1,0:T(4,128)(2,1)S(1)}, bf16[4,19968]{1,0:T(4,128)(2,1)S(1)}, u32[]{:S(2)}, u32[]{:S(2)}) collective-permute-start(bf16[4,19968]{1,0:T(4,128)(2,1)S(1)} %slice_bitcast_fusion), channel_id=1, source_target_pairs={{4,0},{8,4},{12,8},{5,1},{9,5},{13,9},{6,2},{10,6},{14,10},{7,3},{... | collective-permute-start | bytes 479240 | tf_op jit(solution)/shard_map/ppermute | solution.py:236
  3.3 1.3 %fusion.1 = s32[]{:T(128)} fusion(s32[4]{0:T(128)} %param.7, s32[]{:T(128)S(6)} %axis_index.15), kind=kLoop, calls=%fused_computation.9 | loop fusion | flops 11 | bytes 24 | tf_op jit(solution)/shard_map/reduce_sum | solution.py:231
  6.6 4.5 %collective-permute-done = bf16[4,19968]{1,0:T(4,128)(2,1)S(1)} collective-permute-done((bf16[4,19968]{1,0:T(4,128)(2,1)S(1)}, bf16[4,19968]{1,0:T(4,128)(2,1)S(1)}, u32[]{:S(2)}, u32[]{:S(2)}) %collective-permute-start) | collective-permute-done | bytes 159776 | tf_op jit(solution)/shard_map/ppermute | solution.py:236
  11.1 0.1 fusion
  11.2 1.3 %collective-permute-start.1 = (bf16[4,19968]{1,0:T(4,128)(2,1)S(1)}, bf16[4,19968]{1,0:T(4,128)(2,1)S(1)}, u32[]{:S(2)}, u32[]{:S(2)}) collective-permute-start(bf16[4,19968]{1,0:T(4,128)(2,1)S(1)} %fusion), channel_id=1, source_target_pairs={{4,0},{8,4},{12,8},{5,1},{9,5},{13,9},{6,2},{10,6},{14,10},{7,3},{... | collective-permute-start | bytes 479240 | tf_op jit(solution)/shard_map/ppermute | solution.py:237
  12.5 1.3 %copy.14 = bf16[4,4,19968]{2,1,0:T(4,128)(2,1)S(1)} copy(bf16[4,4,19968]{2,0,1:T(4,128)(2,1)} %bitcast.24) | data formatting | bytes 1277952 | tf_op jit(solution)/shard_map/transpose | solution.py:232
  13.8 1.0 %reshape.48.x_ref = bf16[16,19968]{1,0:T(8,128)(2,1)} reshape(bf16[4,4,19968]{2,1,0:T(4,128)(2,1)S(1)} %copy.14) | data formatting | bytes 1277952 | tf_op jit(solution)/shard_map/reshape | solution.py:232
  14.8 0.6 iota_compare_fusion
  15.4 2.9 %collective-permute-done.1 = bf16[4,19968]{1,0:T(4,128)(2,1)S(1)} collective-permute-done((bf16[4,19968]{1,0:T(4,128)(2,1)S(1)}, bf16[4,19968]{1,0:T(4,128)(2,1)S(1)}, u32[]{:S(2)}, u32[]{:S(2)}) %collective-permute-start.1) | collective-permute-done | bytes 159776 | tf_op jit(solution)/shard_map/ppermute | solution.py:237
  18.3 0.8 %select_select_fusion = bf16[6,4,19968]{2,1,0:T(4,128)(2,1)S(1)} fusion(bf16[4,4,19968]{2,1,0:T(4,128)(2,1)S(1)} %bitcast.22, pred[6]{0:T(512)(128)(4,1)S(1)} %get-tuple-element.9, pred[6]{0:T(512)(128)(4,1)S(1)} %get-tuple-element.10, pred[6]{0:T(512)(128)(4,1)S(1)} %iota_compare_fusion.2, bf16[4,19968]{1,0:T(4,128)(2,1)S(1)} %collective-permute-done, ...), kind=kLoop, calls=%fused_computation | loop fusion | flops 1437696 | bytes 1916946 | tf_op jit(solution)/shard_map/jit(_where)/select_n | solution.py:242
  19.1 1.2 %reshape.50.own_ref = bf16[24,19968]{1,0:T(8,128)(2,1)} reshape(bf16[6,4,19968]{2,1,0:T(4,128)(2,1)S(1)} %select_select_fusion) | data formatting | bytes 1916928 | tf_op jit(solution)/shard_map/reshape | solution.py:243
  20.3 0.7 broadcast_in_dim.51.mask_ref
  21.0 48.2 %fused.1 = (bf16[16,19968]{1,0:T(8,128)(2,1)}, f32[3,48,432]{2,1,0:T(8,128)}) custom-call(bf16[16,19968]{1,0:T(8,128)(2,1)} %reshape.48.x_ref, f32[16,192]{1,0:T(8,128)} %broadcast_in_dim.51.mask_ref, bf16[24,19968]{1,0:T(8,128)(2,1)} %reshape.50.own_ref, bf16[27,192,192]{2,1,0:T(8,128)(2,1)} %kern_ref.1), custom_call_target="tpu_custom_call" | custom-call | tf_op jit(solution)/shard_map/fused/pallas_call | solution.py:254
  69.2 0.0 copy-start
  69.3 1.1 %fusion.2 = (f32[1,48,432]{2,1,0:T(8,128)S(1)}, f32[1,48,432]{2,1,0:T(8,128)S(1)}, f32[1,48,432]{2,1,0:T(8,128)S(1)}) fusion(f32[3,48,432]{2,1,0:T(8,128)} %get-tuple-element.5), kind=kLoop, calls=%fused_computation.13 | loop fusion | bytes 497664 | tf_op jit(solution)/shard_map/slice | solution.py:284
  70.3 0.2 slice.27
  70.5 0.2 slice.29
  70.7 0.2 slice.31
  70.9 0.2 maximum_bitcast_fusion
  71.1 0.9 %copy.17 = f32[3,3,3,48,48]{4,3,2,1,0:T(8,128)} copy(f32[3,3,3,48,48]{4,0,2,3,1:T(4,128)S(1)} %maximum_bitcast_fusion) | data formatting | bytes 497664 | tf_op jit(solution)/shard_map/transpose | solution.py:285
  72.0 0.0 copy-done
  72.0 0.1 reshape.51
  72.2 1.1 %copy.20 = bf16[4,4,1,19968]{3,0,2,1:T(4,128)(2,1)} copy(bf16[4,4,1,19968]{3,1,0,2:T(4,128)(2,1)S(1)} %reshape.51) | data formatting | bytes 1277952 | tf_op jit(solution)/shard_map/reshape | solution.py:286
  (2 shorter events, 0.0 us)
Async XLA Ops:
  2.0 9.0 %collective-permute-start = (bf16[4,19968]{1,0:T(4,128)(2,1)S(1)}, bf16[4,19968]{1,0:T(4,128)(2,1)S(1)}, u32[]{:S(2)}, u32[]{:S(2)}) collective-permute-start(bf16[4,19968]{1,0:T(4,128)(2,1)S(1)} %slice_bitcast_fusion), channel_id=1, source_target_pairs={{4,0},{8,4},{12,8},{5,1},{9,5},{13,9},{6,2},{10,6},{14,10},{7,3},{... | collective-permute-start | bytes 479240 | tf_op jit(solution)/shard_map/ppermute | solution.py:236
  11.2 7.2 %collective-permute-start.1 = (bf16[4,19968]{1,0:T(4,128)(2,1)S(1)}, bf16[4,19968]{1,0:T(4,128)(2,1)S(1)}, u32[]{:S(2)}, u32[]{:S(2)}) collective-permute-start(bf16[4,19968]{1,0:T(4,128)(2,1)S(1)} %fusion), channel_id=1, source_target_pairs={{4,0},{8,4},{12,8},{5,1},{9,5},{13,9},{6,2},{10,6},{14,10},{7,3},{... | collective-permute-start | bytes 479240 | tf_op jit(solution)/shard_map/ppermute | solution.py:237
  69.2 2.8 %copy-start = (bf16[16,19968]{1,0:T(8,128)(2,1)S(1)}, bf16[16,19968]{1,0:T(8,128)(2,1)}, u32[]{:S(2)}) copy-start(bf16[16,19968]{1,0:T(8,128)(2,1)} %get-tuple-element.4) | copy-start | bytes 1916932

commit v5 on v4

--- a/solution.py
+++ b/solution.py
@@ -16,7 +16,7 @@
 
 def kernel_body(cells, strips, spans, factor, x_ref, mask_ref, own_ref, kern_ref,
                 out_ref, share_ref, xc, act, act3, gc, wg, got1, send2, got2,
-                zfull, zsend, got3, near, s1, r1, s2, r2, s3, r3, sn, rn):
+                zfull, zsend, got3, near, kern, sk, s1, r1, s2, r2, s3, r3, sn, rn):
     frames = x_ref.shape[0]
     tail = own_ref.shape[0] - frames
     batch = tail // 2
@@ -50,6 +50,8 @@
     pl.when(has_above)(near_copies[0].start)
     pl.when(has_below)(near_copies[1].start)
 
+    kern_copy = pltpu.make_async_copy(kern_ref, kern, sk)
+    kern_copy.start()
     live = mask_ref[...] > 0.5
 
     def split(p, carry):
@@ -83,13 +85,13 @@
         act[end] = zero
         for k in range(9):
             gc[k, end] = zero
-    lax.fori_loop(0, pairs, split, 0)
+    lax.fori_loop(0, pairs, split, 0, unroll=2)
 
     def widen(w, carry):
         act3[w] = jnp.concatenate([act[w], act[w + 1], act[w + 2]], axis=1)
         return carry
 
-    lax.fori_loop(0, cells, widen, 0)
+    lax.fori_loop(0, cells, widen, 0, unroll=4)
     order = list(range(1, half)) + [0]
     copies1, copies2, copies3 = {}, {}, {}
 
@@ -167,7 +169,7 @@
             for c in range(3):
                 g = gc[k, pl.ds(w0 + 2 - c, step)].reshape(step * frames, CH)
                 acc = acc + lax.dot_general(
-                    g, kern_ref[9 * (k % 3) + 3 * (1, 0, 2)[k // 3] + c], (((1,), (1,)), ((), ())), preferred_element_type=jnp.float32
+                    g, kern[9 * (k % 3) + 3 * (1, 0, 2)[k // 3] + c], (((1,), (1,)), ((), ())), preferred_element_type=jnp.float32
                 )
         acc = acc.reshape(step, frames, CH)
         xf = xc[pl.ds(w0, step)].astype(jnp.float32)
@@ -180,7 +182,6 @@
 
     lax.fori_loop(*CUTS[0], weight, 0)
     start_core(0)
-    start_rows(0)
 
     @pl.when(has_below)
     def _():
@@ -203,19 +204,22 @@
     def _():
         near[1] = jnp.zeros(near.shape[1:], near.dtype)
 
-    lax.fori_loop(0, pairs, split_near, 0)
+    lax.fori_loop(0, pairs, split_near, 0, unroll=2)
+    start_rows(0)
     lax.fori_loop(*CUTS[1], weight, 0)
     start_core(1)
-    start_spans(0)
     lax.fori_loop(*CUTS[2], weight, 0)
     start_core(2)
     start_rows(1)
+    start_spans(0)
+    kern_copy.wait()
     lax.fori_loop(0, steps // 4, adjoint, 0)
     start_rows(2)
-    lax.fori_loop(steps // 4, 3 * steps // 4, adjoint, 0)
+    lax.fori_loop(steps // 4, steps // 2, adjoint, 0)
     start_spans(1)
+    lax.fori_loop(steps // 2, 3 * steps // 4, adjoint, 0)
+    start_spans(2)
     lax.fori_loop(3 * steps // 4, steps, adjoint, 0)
-    start_spans(2)
     for n in range(3):
         finish(n)
 
@@ -257,7 +261,7 @@
             jax.ShapeDtypeStruct((frames, flat), jnp.bfloat16),
             jax.ShapeDtypeStruct((3,) + zblock, jnp.float32),
         ),
-        in_specs=[vmem] * 4,
+        in_specs=[vmem] * 3 + [pl.BlockSpec(memory_space=pl.ANY)],
         out_specs=(vmem, vmem),
         scratch_shapes=[
             pltpu.VMEM((cells, frames, CH), jnp.bfloat16),
@@ -272,6 +276,7 @@
             pltpu.VMEM((3, spans) + zblock, jnp.bfloat16),
             pltpu.VMEM((3, some) + zblock, jnp.bfloat16),
             pltpu.VMEM((2, frames + 2 * batch, flat), jnp.bfloat16),
+            pltpu.VMEM(kernel.shape, kernel.dtype), dma(()),
             dma((3, half)), dma((3, half)), dma((3, few)), dma((3, few)), dma((3, some)), dma((3, some)),
             dma((2,)), dma((2,)),
         ],

time: 73.6 us -> 68.4 us (0.929)
  Pallas kernels: 48.2 us -> 43.1 us
    pallas_call x1, Pallas kernels: 48.2 us -> 43.1 us  [body(): pl.pallas_call(functools.partial(kernel_body, cells, strips, spans, float...]
where the time goes in v5:
time: 68.4 us; the launch traced here: 68.1 us
  Pallas kernels  43.1 us (63%)
  local copies, waits for them, and re-layouts  9.27 us (14%)
  waiting for transfers between devices  7.38 us (11%)
  other arithmetic  3.06 us (4%)
  between operations  2.7 us (4%)
  starting transfers between devices  2.58 us (4%)
    pallas_call x1, Pallas kernels, body(): pl.pallas_call(functools.partial(kernel_body, cells, strips, spans, float...  43.1 us
    ppermute x1, waiting for transfers between devices, body(): after_one = lax.ppermute(cot[0], 'tm', back)  4.48 us
    ppermute x1, waiting for transfers between devices, body(): lax.ppermute(jnp.where(count >= 2, cot[1], after_one), 'tm', back)  2.9 us
    slice x4, local copies, waits for them, and re-layouts, body(): share = jnp.stack([share[1], share[0], share[2]])  1.6 us
  transfers between devices with their start and end apart: 2, of which 2 were waited for; matrix products, arithmetic and copies ran while one was open for 6% of the time, Pallas kernels for 0%

profile of v5, /device:TPU:0, one launch (start us, length us, event | category | flops | bytes accessed | tf_op | source)
XLA Modules:
  0.0 68.1 jit_solution(15443626584161573144)
XLA Ops:
  0.6 1.3 %copy.21 = bf16[4,4,1,19968]{3,0,1,2:T(4,128)(2,1)S(1)} copy(bf16[4,4,1,19968]{3,1,2,0:T(4,128)(2,1)} %param.5) | data formatting | bytes 1277952 | tf_op args[1]
  2.0 0.1 slice_bitcast_fusion
  2.0 1.3 %collective-permute-start = (bf16[4,19968]{1,0:T(4,128)(2,1)S(1)}, bf16[4,19968]{1,0:T(4,128)(2,1)S(1)}, u32[]{:S(2)}, u32[]{:S(2)}) collective-permute-start(bf16[4,19968]{1,0:T(4,128)(2,1)S(1)} %slice_bitcast_fusion), channel_id=1, source_target_pairs={{4,0},{8,4},{12,8},{5,1},{9,5},{13,9},{6,2},{10,6},{14,10},{7,3},{... | collective-permute-start | bytes 479240 | tf_op jit(solution)/shard_map/ppermute | solution.py:240
  3.3 1.3 %fusion.1 = s32[]{:T(128)} fusion(s32[4]{0:T(128)} %param.7, s32[]{:T(128)S(6)} %axis_index.15), kind=kLoop, calls=%fused_computation.9 | loop fusion | flops 11 | bytes 24 | tf_op jit(solution)/shard_map/reduce_sum | solution.py:235
  6.6 4.5 %collective-permute-done = bf16[4,19968]{1,0:T(4,128)(2,1)S(1)} collective-permute-done((bf16[4,19968]{1,0:T(4,128)(2,1)S(1)}, bf16[4,19968]{1,0:T(4,128)(2,1)S(1)}, u32[]{:S(2)}, u32[]{:S(2)}) %collective-permute-start) | collective-permute-done | bytes 159776 | tf_op jit(solution)/shard_map/ppermute | solution.py:240
  11.1 0.1 fusion
  11.2 1.3 %collective-permute-start.1 = (bf16[4,19968]{1,0:T(4,128)(2,1)S(1)}, bf16[4,19968]{1,0:T(4,128)(2,1)S(1)}, u32[]{:S(2)}, u32[]{:S(2)}) collective-permute-start(bf16[4,19968]{1,0:T(4,128)(2,1)S(1)} %fusion), channel_id=1, source_target_pairs={{4,0},{8,4},{12,8},{5,1},{9,5},{13,9},{6,2},{10,6},{14,10},{7,3},{... | collective-permute-start | bytes 479240 | tf_op jit(solution)/shard_map/ppermute | solution.py:241
  12.5 1.3 %copy.14 = bf16[4,4,19968]{2,1,0:T(4,128)(2,1)S(1)} copy(bf16[4,4,19968]{2,0,1:T(4,128)(2,1)} %bitcast.24) | data formatting | bytes 1277952 | tf_op jit(solution)/shard_map/transpose | solution.py:236
  13.8 1.0 %reshape.48.x_ref = bf16[16,19968]{1,0:T(8,128)(2,1)} reshape(bf16[4,4,19968]{2,1,0:T(4,128)(2,1)S(1)} %copy.14) | data formatting | bytes 1277952 | tf_op jit(solution)/shard_map/reshape | solution.py:236
  14.8 0.6 iota_compare_fusion
  15.4 2.9 %collective-permute-done.1 = bf16[4,19968]{1,0:T(4,128)(2,1)S(1)} collective-permute-done((bf16[4,19968]{1,0:T(4,128)(2,1)S(1)}, bf16[4,19968]{1,0:T(4,128)(2,1)S(1)}, u32[]{:S(2)}, u32[]{:S(2)}) %collective-permute-start.1) | collective-permute-done | bytes 159776 | tf_op jit(solution)/shard_map/ppermute | solution.py:241
  18.3 0.8 %select_select_fusion = bf16[6,4,19968]{2,1,0:T(4,128)(2,1)S(1)} fusion(bf16[4,4,19968]{2,1,0:T(4,128)(2,1)S(1)} %bitcast.22, pred[6]{0:T(512)(128)(4,1)S(1)} %get-tuple-element.9, pred[6]{0:T(512)(128)(4,1)S(1)} %get-tuple-element.10, pred[6]{0:T(512)(128)(4,1)S(1)} %iota_compare_fusion.2, bf16[4,19968]{1,0:T(4,128)(2,1)S(1)} %collective-permute-done, ...), kind=kLoop, calls=%fused_computation | loop fusion | flops 1437696 | bytes 1916946 | tf_op jit(solution)/shard_map/jit(_where)/select_n | solution.py:246
  19.1 1.2 %reshape.50.own_ref = bf16[24,19968]{1,0:T(8,128)(2,1)} reshape(bf16[6,4,19968]{2,1,0:T(4,128)(2,1)S(1)} %select_select_fusion) | data formatting | bytes 1916928 | tf_op jit(solution)/shard_map/reshape | solution.py:247
  20.3 0.7 broadcast_in_dim.51.mask_ref
  21.0 43.1 %fused.1 = (bf16[16,19968]{1,0:T(8,128)(2,1)}, f32[3,48,432]{2,1,0:T(8,128)}) custom-call(bf16[16,19968]{1,0:T(8,128)(2,1)} %reshape.48.x_ref, f32[16,192]{1,0:T(8,128)} %broadcast_in_dim.51.mask_ref, bf16[24,19968]{1,0:T(8,128)(2,1)} %reshape.50.own_ref, bf16[27,192,192]{2,1,0:T(8,128)(2,1)} %kern_ref.1), custom_call_target="tpu_custom_call" | custom-call | tf_op jit(solution)/shard_map/fused/pallas_call | solution.py:258
  64.1 0.0 copy-start
  64.1 1.1 %fusion.2 = (f32[1,48,432]{2,1,0:T(8,128)S(1)}, f32[1,48,432]{2,1,0:T(8,128)S(1)}, f32[1,48,432]{2,1,0:T(8,128)S(1)}) fusion(f32[3,48,432]{2,1,0:T(8,128)} %get-tuple-element.5), kind=kLoop, calls=%fused_computation.13 | loop fusion | bytes 497664 | tf_op jit(solution)/shard_map/slice | solution.py:289
  65.2 0.2 slice.27
  65.4 0.2 slice.29
  65.5 0.2 slice.31
  65.7 0.2 maximum_bitcast_fusion
  66.0 0.9 %copy.17 = f32[3,3,3,48,48]{4,3,2,1,0:T(8,128)} copy(f32[3,3,3,48,48]{4,0,2,3,1:T(4,128)S(1)} %maximum_bitcast_fusion) | data formatting | bytes 497664 | tf_op jit(solution)/shard_map/transpose | solution.py:290
  66.8 0.0 copy-done
  66.8 0.1 reshape.51
  67.0 1.1 %copy.20 = bf16[4,4,1,19968]{3,0,2,1:T(4,128)(2,1)} copy(bf16[4,4,1,19968]{3,1,0,2:T(4,128)(2,1)S(1)} %reshape.51) | data formatting | bytes 1277952 | tf_op jit(solution)/shard_map/reshape | solution.py:291
  (2 shorter events, 0.0 us)
Async XLA Ops:
  2.0 9.0 %collective-permute-start = (bf16[4,19968]{1,0:T(4,128)(2,1)S(1)}, bf16[4,19968]{1,0:T(4,128)(2,1)S(1)}, u32[]{:S(2)}, u32[]{:S(2)}) collective-permute-start(bf16[4,19968]{1,0:T(4,128)(2,1)S(1)} %slice_bitcast_fusion), channel_id=1, source_target_pairs={{4,0},{8,4},{12,8},{5,1},{9,5},{13,9},{6,2},{10,6},{14,10},{7,3},{... | collective-permute-start | bytes 479240 | tf_op jit(solution)/shard_map/ppermute | solution.py:240
  11.2 7.2 %collective-permute-start.1 = (bf16[4,19968]{1,0:T(4,128)(2,1)S(1)}, bf16[4,19968]{1,0:T(4,128)(2,1)S(1)}, u32[]{:S(2)}, u32[]{:S(2)}) collective-permute-start(bf16[4,19968]{1,0:T(4,128)(2,1)S(1)} %fusion), channel_id=1, source_target_pairs={{4,0},{8,4},{12,8},{5,1},{9,5},{13,9},{6,2},{10,6},{14,10},{7,3},{... | collective-permute-start | bytes 479240 | tf_op jit(solution)/shard_map/ppermute | solution.py:241
  64.1 2.8 %copy-start = (bf16[16,19968]{1,0:T(8,128)(2,1)S(1)}, bf16[16,19968]{1,0:T(8,128)(2,1)}, u32[]{:S(2)}) copy-start(bf16[16,19968]{1,0:T(8,128)(2,1)} %get-tuple-element.4) | copy-start | bytes 1916932
